TPU v7x, 256 devices: a whole 4x4x8 slice. The times are simulated.
256 devices in a mesh: seq: 32 (over x, z_lo, core), head: 8 (over z_hi, y).
Axes of the slice: x: 4, y: 4, z: 8 (z_hi: 2, z_lo: 4; z = z_hi * 4 + z_lo), core: 2. Of those that a mesh axis runs over, the one named last changes fastest.
Arguments:
- normed: bfloat16 [16384, 5376], P('seq'), may hold values from -6 to 6
- cotangent: bfloat16 [16384, 2048], P('seq', 'head'), may hold values from -6 to 6
- qkv_master: float32 [5376, 8, 512], P('seq', 'head'), may hold values from -0.078125 to 0.078125
- adam_first: float32 [5376, 8, 512], P('seq', 'head'), may hold values from -6 to 6
- adam_second: float32 [5376, 8, 512], P('seq', 'head'), may hold values from 0.5 to 20
- skip_flag: int32 [8], replicated, may hold values 0 or 1
- scale_exponent: int32 [1], replicated, may hold values from 4 to 8
Outputs:
- attn_out: bfloat16 [16384, 2048], P('seq', 'head')
- d_tokens: bfloat16 [16384, 5376], P(('seq', 'head'))
- new_master: float32 [5376, 8, 512], P('seq', 'head')
- new_first: float32 [5376, 8, 512], P('seq', 'head')
- new_second: float32 [5376, 8, 512], P('seq', 'head')
All inputs are finite; a program needn't handle non-finite values.
Results may differ from a plain program's by a relative error of at most 0.0095.
Values may be sent and summed in bfloat16 or wider, within the bound.
No kernel may reach another device: no remote copies, remote signals or barrier semaphores. Data moves between devices by JAX's collectives and lax.ppermute only.
A program may use at most 128 MiB of HBM per device.

v0:
```python
import jax
import jax.numpy as jnp
from jax import lax
from jax.experimental import pallas as pl
from jax.experimental.pallas import tpu as pltpu
from jax.sharding import PartitionSpec as P

HEAD_DIM = 128
ATTEND_SPAN = 1024
ATTN_SCALAR = 168
ADAM_STEP = 1000

norm_eps = 1e-06
beta_one = 0.9
beta_two = 0.95
adam_eps = 1e-08
learn_rate = 0.01
weight_decay = 0.1

bf16 = jnp.bfloat16
f32 = jnp.float32

SEQ = 32
HEAD = 8


def seq_move(block, dx=0, dz=0, swap=False):
    pairs = []
    for s in range(SEQ):
        x, z, c = s // 8, (s // 2) % 4, s % 2
        pairs.append((s, ((x + dx) % 4) * 8 + ((z + dz) % 4) * 2 + (c ^ int(swap))))
    return lax.ppermute(block, "seq", pairs)


def head_move(block, dy=0, flip=False):
    pairs = []
    for h in range(HEAD):
        half, y = h // 4, h % 4
        pairs.append((h, (half ^ int(flip)) * 4 + (y + dy) % 4))
    return lax.ppermute(block, "head", pairs)


def swap_cores(block):
    return seq_move(block, swap=True)


def shifted(block, distance):
    route = [(i - distance, i) for i in range(SEQ) if 0 <= i - distance < SEQ]
    return lax.ppermute(block, "seq", route)


def tie(later, *earlier):
    return lax.optimization_barrier((later,) + earlier)[0]


def place(blocks, spots):
    out = jnp.broadcast_to(blocks[0][None], (4,) + blocks[0].shape)
    for block, spot in zip(blocks[1:], spots[1:]):
        out = lax.dynamic_update_slice(out, block[None], (spot,) + (0,) * block.ndim)
    return out.reshape((-1,) + blocks[0].shape[1:])


def gather_z(block, z):
    parts = [block] + [seq_move(block, dz=k) for k in (1, 2, 3)]
    return place(parts, [(z - k) % 4 for k in range(4)])


def spread_x(block):
    return [seq_move(block, dx=k) for k in (1, 3, 2)]


def join_x(block, parts, x):
    return place([block] + parts, [x, (x - 1) % 4, (x + 1) % 4, (x + 2) % 4])


def send_parts(total, pos, move):
    blocks = total.reshape(4, -1, total.shape[1])
    pick = lambda k: lax.dynamic_index_in_dim(blocks, (pos + k) % 4, 0, keepdims=False)
    return [pick(0)] + [move(pick(k), k) for k in (1, 3, 2)]


def add_parts(parts):
    return sum(p.astype(f32) for p in parts[1:]) + parts[0].astype(f32)


def head_norm(raw_vals):
    factor = lax.rsqrt(jnp.mean(raw_vals * raw_vals, axis=-1, keepdims=True) + norm_eps)
    return (raw_vals * factor, factor)


def norm_back(raw_vals, factor, grad_in):
    inner_mean = jnp.mean(raw_vals * grad_in, axis=-1, keepdims=True)
    return factor * grad_in - raw_vals * factor * factor * factor * inner_mean


def pair_cols(even, a, b):
    return jnp.where(even, a, b), jnp.where(even, b, a)


def rows_pair(even, mine, theirs):
    return jnp.where(even, jnp.concatenate([mine, theirs], 0), jnp.concatenate([theirs, mine], 0))


def nt(a, b):
    return lax.dot_general(a, b, (((1,), (1,)), ((), ())), preferred_element_type=f32)


def tn(a, b):
    return lax.dot_general(a, b, (((0,), (0,)), ((), ())), preferred_element_type=f32)


TILE = 896


def near():
    return pl.BlockSpec(memory_space=pltpu.VMEM)


def limit(mib):
    return pltpu.CompilerParams(vmem_limit_bytes=mib << 20)


def term_kernel(n_ref, g_ref, keep_ref, send_ref, turned):
    turned[...] = g_ref[...].T

    @pl.loop(0, n_ref.shape[1] // TILE)
    def _(i):
        spot = pl.ds(pl.multiple_of(i * TILE, TILE), TILE)
        out = jnp.dot(turned[...], n_ref[:, spot], preferred_element_type=f32).astype(bf16).T
        keep_ref[spot, :] = out[:, :HEAD_DIM]
        send_ref[spot, :] = out[:, HEAD_DIM:]


def weight_terms(normed, pair):
    rows, width = normed.shape
    shape = jax.ShapeDtypeStruct((width, HEAD_DIM), bf16)
    return pl.pallas_call(
        term_kernel,
        in_specs=[near(), near()],
        out_specs=[near(), near()],
        out_shape=[shape, shape],
        scratch_shapes=[pltpu.VMEM((2 * HEAD_DIM, rows), bf16)],
        compiler_params=limit(8),
        name="weight_terms",
    )(normed, pair)


def tokens_kernel(own_ref, far_ref, ka_ref, kb_ref, qa_ref, qb_ref, fa_ref, fb_ref, o_ref, turned):
    hd = HEAD_DIM
    turned[: 4 * hd] = own_ref[...].T
    turned[4 * hd :] = far_ref[...].T

    @pl.loop(0, o_ref.shape[1] // TILE)
    def _(i):
        spot = pl.ds(pl.multiple_of(i * TILE, TILE), TILE)
        rows = jnp.concatenate(
            [ka_ref[spot, :], kb_ref[spot, :], qa_ref[spot, :], qb_ref[spot, :],
             fa_ref[spot, :hd], fb_ref[spot, :hd], fa_ref[spot, hd:], fb_ref[spot, hd:]], 1)
        acc = jnp.dot(rows, turned[...], preferred_element_type=f32)
        o_ref[:, spot] = acc.astype(bf16).T


def token_terms(own, far, narrow, wide):
    rows, cols = own.shape
    width = wide[0].shape[0]
    return pl.pallas_call(
        tokens_kernel,
        in_specs=[near()] * 8,
        out_specs=near(),
        out_shape=jax.ShapeDtypeStruct((rows, width), bf16),
        scratch_shapes=[pltpu.VMEM((2 * cols, rows), bf16)],
        compiler_params=limit(12),
        name="token_terms",
    )(own, far, *narrow, *wide)


Q_TILE = 256


def attend_kernel(pos_ref, power_ref, q_ref, two_ref, one_ref, own_ref, cot_ref,
                  out_ref, gq_ref, two_out, one_out, own_out, ext, acc):
    hd = HEAD_DIM
    rows = own_ref.shape[0]
    step = pl.program_id(0)
    start = pl.multiple_of((step // 2) * Q_TILE, Q_TILE)
    span = ATTEND_SPAN + Q_TILE
    scale = float(ATTN_SCALAR) ** (-0.5)

    @pl.when(step == 0)
    def _():
        ext[:rows] = two_ref[...]
        ext[rows : 2 * rows] = one_ref[...]
        ext[2 * rows :] = own_ref[...]
        acc[...] = jnp.zeros_like(acc)

    q_raw = q_ref[...]
    factor = lax.rsqrt(jnp.mean(q_raw * q_raw, axis=1, keepdims=True) + norm_eps)
    queries = (q_raw * factor).astype(bf16)
    keys = ext[pl.ds(start, span), :hd]
    values = ext[pl.ds(start, span), hd:]
    scores = nt(queries, keys) * scale
    spot = lax.broadcasted_iota(jnp.int32, scores.shape, 1)
    gap = lax.broadcasted_iota(jnp.int32, scores.shape, 0) + ATTEND_SPAN - spot
    first = ATTEND_SPAN - pos_ref[0] * rows - start
    allowed = (gap >= 0) & (gap < ATTEND_SPAN) & (spot >= first)
    kernel = jnp.where(allowed, jnp.exp(scores), 0.0)
    totals = jnp.sum(kernel, axis=1, keepdims=True)
    probs = (kernel / totals).astype(bf16)
    mixed = jnp.dot(probs, values, preferred_element_type=f32)
    out_ref[...] = mixed.astype(bf16)
    grad_out = (cot_ref[...].astype(f32) * power_ref[0]).astype(bf16)
    delta = jnp.sum(grad_out.astype(f32) * mixed, axis=1, keepdims=True)
    grad_probs = nt(grad_out, values)
    grad_scores = (probs.astype(f32) * (grad_probs - delta) * scale).astype(bf16)
    grad_q = jnp.dot(grad_scores, keys, preferred_element_type=f32)
    inner = jnp.mean(q_raw * grad_q, axis=1, keepdims=True)
    gq_ref[...] = (factor * grad_q - q_raw * factor * factor * factor * inner).astype(bf16)
    acc[pl.ds(start, span), :hd] += tn(grad_scores, queries)
    acc[pl.ds(start, span), hd:] += tn(probs, grad_out)

    @pl.when(step == pl.num_programs(0) - 1)
    def _():
        two_out[...] = acc[:rows].astype(bf16)
        one_out[...] = acc[rows : 2 * rows].astype(bf16)
        own_out[...] = acc[2 * rows :]


def attend(pos, power, q_cols, two, one, own, cotangent):
    rows = own.shape[0]
    hd = HEAD_DIM
    whole = pl.BlockSpec((rows, 2 * hd), lambda i, p: (0, 0))
    plain = pl.BlockSpec((Q_TILE, hd), lambda i, p: (i // 2, i % 2))
    turned = pl.BlockSpec((Q_TILE, hd), lambda i, p: (i // 2, (i + p[1]) % 2))
    shape = lambda kind: jax.ShapeDtypeStruct((rows, 2 * hd), kind)
    return pl.pallas_call(
        attend_kernel,
        grid_spec=pltpu.PrefetchScalarGridSpec(
            num_scalar_prefetch=1,
            grid=(2 * rows // Q_TILE,),
            in_specs=[pl.BlockSpec(memory_space=pltpu.SMEM), turned, whole, whole, whole, plain],
            out_specs=[plain, turned, whole, whole, whole],
            scratch_shapes=[
                pltpu.VMEM((ATTEND_SPAN + rows, 2 * hd), bf16),
                pltpu.VMEM((ATTEND_SPAN + rows, 2 * hd), f32),
            ],
        ),
        out_shape=[shape(bf16), shape(bf16), shape(bf16), shape(bf16), shape(f32)],
        compiler_params=limit(24),
        name="attend",
    )(pos, power, q_cols, two, one, own, cotangent)


def step_kernel(info_ref, power_ref, mine_ref, got_ref, master_ref, first_ref, second_ref,
                master_out, first_out, second_out, grads):
    hd = HEAD_DIM
    rows = mine_ref.shape[0]
    even = info_ref[0] == 0
    for k, col in enumerate((1, 1, 0, 0)):
        mine = mine_ref[:, col * hd : (col + 1) * hd]
        got = got_ref[:, col * hd : (col + 1) * hd]
        grads[pl.ds(k, rows, stride=4), :] = jnp.where(even == (k % 2 == 0), mine, got)
    gradient = grads[...] / power_ref[0]
    master, first, second = master_ref[...], first_ref[...], second_ref[...]
    first_new = beta_one * first + (1.0 - beta_one) * gradient
    second_new = beta_two * second + (1.0 - beta_two) * gradient * gradient
    first_fix = 1.0 - beta_one**ADAM_STEP
    second_fix = 1.0 - beta_two**ADAM_STEP
    update = first_new / first_fix / (jnp.sqrt(second_new / second_fix) + adam_eps)
    applied = info_ref[1] == 0
    master_out[...] = jnp.where(
        applied, master - learn_rate * (update + weight_decay * master), master
    )
    first_out[...] = jnp.where(applied, first_new, first)
    second_out[...] = jnp.where(applied, second_new, second)


def adam_step(info, power, mine, got, master, first, second):
    smem = pl.BlockSpec(memory_space=pltpu.SMEM)
    return pl.pallas_call(
        step_kernel,
        in_specs=[smem, smem] + [near()] * 5,
        out_specs=[near()] * 3,
        out_shape=[jax.ShapeDtypeStruct(master.shape, f32)] * 3,
        scratch_shapes=[pltpu.VMEM(master.shape, f32)],
        compiler_params=limit(8),
        name="adam_step",
    )(info, power, mine, got, master, first, second)


def per_device(normed, cotangent, qkv_master, adam_first, adam_second, skip_flag, scale_exponent):
    tok_rows = normed.shape[0]
    hd = HEAD_DIM
    own_rows = qkv_master.shape[0]
    seq_pos = lax.axis_index("seq")
    head_pos = lax.axis_index("head")
    x, z, core = seq_pos // 8, (seq_pos // 2) % 4, seq_pos % 2
    half = head_pos // 4
    even = core == 0

    master16 = qkv_master.reshape(own_rows, 4 * hd).astype(bf16)
    cols = [master16[:, i * hd : (i + 1) * hd] for i in range(4)]
    kv_mine, kv_theirs = pair_cols(even, cols[2], cols[3])
    q_mine, q_theirs = pair_cols(even, cols[0], cols[1])
    got = swap_cores(jnp.concatenate([kv_theirs, q_theirs], 1))
    kv_block = rows_pair(even, kv_mine, got[:, :hd])
    q_block = rows_pair(even, q_mine, got[:, hd:])
    kv_q_block = jnp.concatenate([kv_block, q_block], 1)
    plane = gather_z(kv_q_block, z)
    kv_plane, q_plane = plane[:, :hd], plane[:, hd:]
    kv_parts = spread_x(kv_plane)
    q_parts = spread_x(tie(q_plane, kv_plane))
    far_block = head_move(tie(kv_q_block, plane), flip=True)
    kv_weights = join_x(kv_plane, kv_parts, x)
    kv_other = swap_cores(kv_weights)
    far_plane = gather_z(tie(far_block, kv_weights), z)

    kv = jnp.dot(normed, jnp.concatenate([kv_weights, kv_other], 1), preferred_element_type=f32)
    k_raw, v_raw = pair_cols(even, kv[:, :hd], kv[:, hd:])
    k_unit, k_factor = head_norm(k_raw)
    kv16 = jnp.concatenate([k_unit.astype(bf16), v_raw.astype(bf16)], 1)
    kv_two, kv_one = shifted(kv16, 2), shifted(kv16, 1)

    q_parts = list(lax.optimization_barrier((kv16, *q_parts))[1:])
    q_weights = join_x(q_plane, q_parts, x)
    q_other = swap_cores(q_weights)
    far_plane = tie(far_plane, q_weights)
    far_parts = spread_x(far_plane)

    q_cols = jnp.dot(normed, jnp.concatenate([q_weights, q_other], 1), preferred_element_type=f32)
    scale_power = jnp.left_shift(jnp.int32(1), scale_exponent).astype(f32)
    attn_out, gq_pair, part_two, part_one, part_own = attend(
        jnp.stack([seq_pos, core]), scale_power, tie(q_cols, far_plane),
        kv_two, kv_one, kv16, cotangent,
    )
    back_two, back_one = shifted(part_two, -2), shifted(part_one, -1)

    def weight_sum(pair):
        keep, send = weight_terms(normed, pair)
        got = swap_cores(send)
        return (keep.astype(f32) + got.astype(f32)).astype(bf16)

    move_x = lambda b, k: seq_move(b, dx=k)
    wq_sum = weight_sum(gq_pair)
    wq_parts = send_parts(wq_sum, x, move_x)

    grad_kv = part_own + back_one.astype(f32) + back_two.astype(f32)
    g_k = norm_back(k_raw, k_factor, grad_kv[:, :hd]).astype(bf16)
    g_v = grad_kv[:, hd:].astype(bf16)
    gkv_pair = jnp.concatenate(pair_cols(even, g_k, g_v), 1)
    far_parts = list(lax.optimization_barrier((gkv_pair, *far_parts))[1:])
    far_weights = join_x(far_plane, far_parts, x)
    far_other = swap_cores(far_weights)
    wkv_sum = weight_sum(gkv_pair)
    wkv_parts = send_parts(wkv_sum, x, move_x)

    g_all = jnp.concatenate([gkv_pair, gq_pair], 1)
    own_half = lax.dynamic_slice_in_dim(g_all, half * (tok_rows // 2), tok_rows // 2, 0)
    far_half = lax.dynamic_slice_in_dim(g_all, (1 - half) * (tok_rows // 2), tok_rows // 2, 0)
    got_half = head_move(far_half, flip=True)
    d_part = token_terms(
        own_half,
        got_half,
        (kv_weights, kv_other, q_weights, q_other),
        (far_weights, far_other),
    )
    d_blocks = lax.all_to_all(
        d_part.reshape(4, tok_rows // 8, -1), "head", split_axis=0, concat_axis=0, tiled=True,
        axis_index_groups=[[0, 1, 2, 3], [4, 5, 6, 7]],
    )
    d_tokens = add_parts([d_blocks[k] for k in range(4)]).astype(bf16)

    tied = lax.optimization_barrier((d_part, *wq_parts, *wkv_parts))[1:]
    w_x = jnp.concatenate(
        [add_parts(tied[4:]).astype(bf16), add_parts(tied[:4]).astype(bf16)], 1
    )
    z_parts = send_parts(w_x, z, lambda b, k: seq_move(b, dz=k))
    w_z = add_parts(z_parts)

    mine = lax.dynamic_slice_in_dim(w_z, core * own_rows, own_rows, 0)
    got = swap_cores(lax.dynamic_slice_in_dim(w_z, (1 - core) * own_rows, own_rows, 0))
    flag = lax.dynamic_index_in_dim(skip_flag, head_pos, 0, keepdims=False)
    flat = lambda a: a.reshape(own_rows * 4, hd)
    new = adam_step(
        jnp.stack([core, flag]), scale_power, mine, got,
        flat(qkv_master), flat(adam_first), flat(adam_second),
    )
    return (attn_out, d_tokens) + tuple(a.reshape(qkv_master.shape) for a in new)


def solution(mesh):
    return jax.shard_map(
        per_device,
        mesh=mesh,
        in_specs=(
            P("seq", None),
            P("seq", "head"),
            P("seq", "head", None),
            P("seq", "head", None),
            P("seq", "head", None),
            P(),
            P(),
        ),
        out_specs=(
            P("seq", "head"),
            P(("seq", "head"), None),
            P("seq", "head", None),
            P("seq", "head", None),
            P("seq", "head", None),
        ),
        check_vma=False,
    )
```

profile of v0, /device:TPU:1, one launch (start us, length us, event | category | flops | bytes accessed | tf_op | source)
XLA Modules:
  0.0 223.4 jit_solution(18083180386748219150)
XLA Ops:
  0.6 1.2 convert_element_type.106
  2.0 3.3 %collective-permute-start = (bf16[168,256]{1,0:T(8,128)(2,1)S(1)}, bf16[168,256]{1,0:T(8,128)(2,1)S(1)}, u32[]{:S(2)}, u32[]{:S(2)}) collective-permute-start(bf16[168,256]{1,0:T(8,128)(2,1)S(1)} %pad_maximum_fusion.5), channel_id=1, source_target_pairs={{0,8},{8,0},{16,24},{24,16},{32,40},{40,32},{48,56},{56,48},{64,72... | collective-permute-start | bytes 258056 | tf_op jit(solution)/shard_map/ppermute | solution.py:32
  6.5 2.8 %collective-permute-start.2 = (bf16[336,256]{1,0:T(8,128)(2,1)S(1)}, bf16[336,256]{1,0:T(8,128)(2,1)S(1)}, u32[]{:S(2)}, u32[]{:S(2)}) collective-permute-start(bf16[336,256]{1,0:T(8,128)(2,1)S(1)} %pad_maximum_fusion.4), channel_id=1, source_target_pairs={{0,32},{8,40},{16,48},{24,56},{32,0},{40,8},{48,16},{56,24},{64,96... | collective-permute-start | bytes 516104 | tf_op jit(solution)/shard_map/ppermute | solution.py:32
  10.0 3.8 %collective-permute-done.1 = bf16[336,256]{1,0:T(8,128)(2,1)S(1)} collective-permute-done((bf16[336,256]{1,0:T(8,128)(2,1)S(1)}, bf16[336,256]{1,0:T(8,128)(2,1)S(1)}, u32[]{:S(2)}, u32[]{:S(2)}) %collective-permute-start.1) | collective-permute-done | bytes 172064 | tf_op jit(solution)/shard_map/ppermute | solution.py:32
  13.8 7.3 %collective-permute-done.2 = bf16[336,256]{1,0:T(8,128)(2,1)S(1)} collective-permute-done((bf16[336,256]{1,0:T(8,128)(2,1)S(1)}, bf16[336,256]{1,0:T(8,128)(2,1)S(1)}, u32[]{:S(2)}, u32[]{:S(2)}) %collective-permute-start.2) | collective-permute-done | bytes 172064 | tf_op jit(solution)/shard_map/ppermute | solution.py:32
  21.3 1.3 collective-permute-start.4
  22.6 1.4 collective-permute-start.5
  24.1 1.6 collective-permute-start.6
  25.6 5.3 %collective-permute-done.4 = bf16[1344,128]{1,0:T(8,128)(2,1)S(1)} collective-permute-done((bf16[1344,128]{1,0:T(8,128)(2,1)S(1)}, bf16[1344,128]{1,0:T(8,128)(2,1)S(1)}, u32[]{:S(2)}, u32[]{:S(2)}) %collective-permute-start.4) | collective-permute-done | bytes 344096 | tf_op jit(solution)/shard_map/ppermute | solution.py:32
  31.5 8.6 %collective-permute-done.6 = bf16[1344,128]{1,0:T(8,128)(2,1)S(1)} collective-permute-done((bf16[1344,128]{1,0:T(8,128)(2,1)S(1)}, bf16[1344,128]{1,0:T(8,128)(2,1)S(1)}, u32[]{:S(2)}, u32[]{:S(2)}) %collective-permute-start.6) | collective-permute-done | bytes 344096 | tf_op jit(solution)/shard_map/ppermute | solution.py:32
  40.1 1.5 collective-permute-start.7
  42.5 1.8 collective-permute-start.9
  44.5 4.6 %fusion.11 = f32[512,256]{1,0:T(8,128)S(1)} fusion(bf16[512,5376]{1,0:T(8,128)(2,1)} %n_ref.3, bf16[5376,128]{1,0:T(8,128)(2,1)S(1)} %collective-permute-done.7.kb_ref, bf16[5376,128]{1,0:T(8,128)(2,1)S(1)} %bitcast.91), kind=kOutput, calls=%fused_computation.12 | convolution fusion | flops 1414791168 | bytes 8781824 | tf_op jit(solution)/shard_map/dot_general | solution.py:317
  49.6 2.7 %collective-permute-done.8 = bf16[1344,128]{1,0:T(8,128)(2,1)S(1)} collective-permute-done((bf16[1344,128]{1,0:T(8,128)(2,1)S(1)}, bf16[1344,128]{1,0:T(8,128)(2,1)S(1)}, u32[]{:S(2)}, u32[]{:S(2)}) %collective-permute-start.8) | collective-permute-done | bytes 344096 | tf_op jit(solution)/shard_map/ppermute | solution.py:32
  52.3 7.6 %collective-permute-done.10 = bf16[1344,128]{1,0:T(8,128)(2,1)S(1)} collective-permute-done((bf16[1344,128]{1,0:T(8,128)(2,1)S(1)}, bf16[1344,128]{1,0:T(8,128)(2,1)S(1)}, u32[]{:S(2)}, u32[]{:S(2)}) %collective-permute-start.10) | collective-permute-done | bytes 344096 | tf_op jit(solution)/shard_map/ppermute | solution.py:32
  60.3 1.0 collective-permute-start.11
  61.4 5.6 %collective-permute-start.12 = (bf16[336,256]{1,0:T(8,128)(2,1)S(1)}, bf16[336,256]{1,0:T(8,128)(2,1)S(1)}, u32[]{:S(2)}, u32[]{:S(2)}) collective-permute-start(bf16[336,256]{1,0:T(8,128)(2,1)S(1)} %pad_maximum_fusion.4), channel_id=1, source_target_pairs={{0,4},{1,5},{2,6},{3,7},{4,0},{5,1},{6,2},{7,3},{8,12},{9,13},{10,... | collective-permute-start | bytes 516104 | tf_op jit(solution)/shard_map/ppermute | solution.py:40
  66.9 4.6 %collective-permute-done.12 = bf16[336,256]{1,0:T(8,128)(2,1)S(1)} collective-permute-done((bf16[336,256]{1,0:T(8,128)(2,1)S(1)}, bf16[336,256]{1,0:T(8,128)(2,1)S(1)}, u32[]{:S(2)}, u32[]{:S(2)}) %collective-permute-start.12) | collective-permute-done | bytes 172064 | tf_op jit(solution)/shard_map/ppermute | solution.py:40
  71.5 7.8 %collective-permute-start.13 = (bf16[336,256]{1,0:T(8,128)(2,1)S(1)}, bf16[336,256]{1,0:T(8,128)(2,1)S(1)}, u32[]{:S(2)}, u32[]{:S(2)}) collective-permute-start(bf16[336,256]{1,0:T(8,128)(2,1)S(1)} %collective-permute-done.12), channel_id=1, source_target_pairs={{0,16},{8,24},{16,32},{24,40},{32,48},{40,56},{48,0},{56,8},{64,80... | collective-permute-start | bytes 516104 | tf_op jit(solution)/shard_map/ppermute | solution.py:32
  80.2 2.1 collective-permute-start.15
  82.6 8.3 %collective-permute-done.14 = bf16[336,256]{1,0:T(8,128)(2,1)S(1)} collective-permute-done((bf16[336,256]{1,0:T(8,128)(2,1)S(1)}, bf16[336,256]{1,0:T(8,128)(2,1)S(1)}, u32[]{:S(2)}, u32[]{:S(2)}) %collective-permute-start.14) | collective-permute-done | bytes 172064 | tf_op jit(solution)/shard_map/ppermute | solution.py:32
  90.9 5.9 %collective-permute-start.16 = (bf16[512,256]{1,0:T(8,128)(2,1)S(1)}, bf16[512,256]{1,0:T(8,128)(2,1)S(1)}, u32[]{:S(2)}, u32[]{:S(2)}) collective-permute-start(bf16[512,256]{1,0:T(8,128)(2,1)S(1)} %pad_maximum_fusion.2.own_ref), channel_id=1, source_target_pairs={{0,16},{8,24},{16,32},{24,40},{32,48},{40,56},{48,64},{56,72},{64,... | collective-permute-start | bytes 786440 | tf_op jit(solution)/shard_map/ppermute | solution.py:49
  96.8 2.3 %collective-permute-start.17 = (bf16[512,256]{1,0:T(8,128)(2,1)S(1)}, bf16[512,256]{1,0:T(8,128)(2,1)S(1)}, u32[]{:S(2)}, u32[]{:S(2)}) collective-permute-start(bf16[512,256]{1,0:T(8,128)(2,1)S(1)} %pad_maximum_fusion.2.own_ref), channel_id=1, source_target_pairs={{0,8},{8,16},{16,24},{24,32},{32,40},{40,48},{48,56},{56,64},{64,7... | collective-permute-start | bytes 786440 | tf_op jit(solution)/shard_map/ppermute | solution.py:49
  99.1 1.6 fusion.8.q_ref
  100.7 1.2 collective-permute-done.16.two_ref
  101.9 3.8 %collective-permute-done.17.one_ref = bf16[512,256]{1,0:T(8,128)(2,1)S(1)} collective-permute-done((bf16[512,256]{1,0:T(8,128)(2,1)S(1)}, bf16[512,256]{1,0:T(8,128)(2,1)S(1)}, u32[]{:S(2)}, u32[]{:S(2)}) %collective-permute-start.17) | collective-permute-done | bytes 262176 | tf_op jit(solution)/shard_map/ppermute | solution.py:49
  105.7 8.2 %attend.1 = (bf16[512,256]{1,0:T(8,128)(2,1)}, bf16[512,256]{1,0:T(8,128)(2,1)S(1)}, bf16[512,256]{1,0:T(8,128)(2,1)S(1)}, bf16[512,256]{1,0:T(8,128)(2,1)S(1)}, f32[512,256]{1,0:T(8,128)S(1)}) custom-call(s32[2]{0:T(128)S(1)} %pad_add_fusion.pos_ref, f32[1]{0:T(128)S(6)} %convert_element_type.105.power_ref, f32[512,256]{1,0:T(8,128)S(1)} %fusion.8.q_ref, ...), custom_call_target="tpu_custom_call" | custom-call | tf_op jit(solution)/shard_map/attend/pallas_call | solution.py:235
  113.9 1.3 collective-permute-start.19
  115.2 1.9 collective-permute-start.18
  117.1 6.6 %collective-permute-start.21 = (bf16[1344,256]{1,0:T(8,128)(2,1)S(1)}, bf16[1344,256]{1,0:T(8,128)(2,1)S(1)}, u32[]{:S(2)}, u32[]{:S(2)}) collective-permute-start(bf16[1344,256]{1,0:T(8,128)(2,1)S(1)} %bitcast.100), channel_id=1, source_target_pairs={{0,64},{8,72},{16,80},{24,88},{32,96},{40,104},{48,112},{56,120},{... | collective-permute-start | bytes 2064392 | tf_op jit(solution)/shard_map/ppermute | solution.py:32
  123.8 2.6 %collective-permute-start.23 = (bf16[1344,256]{1,0:T(8,128)(2,1)S(1)}, bf16[1344,256]{1,0:T(8,128)(2,1)S(1)}, u32[]{:S(2)}, u32[]{:S(2)}) collective-permute-start(bf16[1344,256]{1,0:T(8,128)(2,1)S(1)} %bitcast.102), channel_id=1, source_target_pairs={{0,128},{8,136},{16,144},{24,152},{32,160},{40,168},{48,176},{56,1... | collective-permute-start | bytes 2064392 | tf_op jit(solution)/shard_map/ppermute | solution.py:32
  126.4 2.6 %copy-done = bf16[512,5376]{1,0:T(8,128)(2,1)S(1)} copy-done((bf16[512,5376]{1,0:T(8,128)(2,1)S(1)}, bf16[512,5376]{1,0:T(8,128)(2,1)}, u32[]{:S(2)}) %copy-start) | copy-done | bytes 5505048
  129.0 3.2 %weight_terms.2 = (bf16[5376,128]{1,0:T(8,128)(2,1)S(1)}, bf16[5376,128]{1,0:T(8,128)(2,1)S(1)}) custom-call(bf16[512,5376]{1,0:T(8,128)(2,1)S(1)} %copy-done, bf16[512,256]{1,0:T(8,128)(2,1)S(1)} %get-tuple-element.48.g_ref), custom_call_target="tpu_custom_call" | custom-call | tf_op jit(solution)/shard_map/weight_terms/pallas_call | solution.py:137
  132.2 0.9 collective-permute-start.25
  133.7 5.2 %collective-permute-start.20 = (bf16[256,512]{1,0:T(8,128)(2,1)S(1)}, bf16[256,512]{1,0:T(8,128)(2,1)S(1)}, u32[]{:S(2)}, u32[]{:S(2)}) collective-permute-start(bf16[256,512]{1,0:T(8,128)(2,1)S(1)} %get-tuple-element.89), channel_id=1, source_target_pairs={{0,4},{1,5},{2,6},{3,7},{4,0},{5,1},{6,2},{7,3},{8,12},{9,13},{10,... | collective-permute-start | bytes 786440 | tf_op jit(solution)/shard_map/ppermute | solution.py:40
  139.0 2.6 %copy-done.1 = bf16[512,5376]{1,0:T(8,128)(2,1)S(1)} copy-done((bf16[512,5376]{1,0:T(8,128)(2,1)S(1)}, bf16[512,5376]{1,0:T(8,128)(2,1)}, u32[]{:S(2)}) %copy-start.1) | copy-done | bytes 5505048
  141.6 3.2 %weight_terms.3 = (bf16[5376,128]{1,0:T(8,128)(2,1)S(1)}, bf16[5376,128]{1,0:T(8,128)(2,1)S(1)}) custom-call(bf16[512,5376]{1,0:T(8,128)(2,1)S(1)} %copy-done.1, bf16[512,256]{1,0:T(8,128)(2,1)S(1)} %pad_maximum_fusion.3.g_ref), custom_call_target="tpu_custom_call" | custom-call | tf_op jit(solution)/shard_map/weight_terms/pallas_call | solution.py:137
  144.8 10.7 %collective-permute-done.23 = bf16[1344,256]{1,0:T(8,128)(2,1)S(1)} collective-permute-done((bf16[1344,256]{1,0:T(8,128)(2,1)S(1)}, bf16[1344,256]{1,0:T(8,128)(2,1)S(1)}, u32[]{:S(2)}, u32[]{:S(2)}) %collective-permute-start.23) | collective-permute-done | bytes 688160 | tf_op jit(solution)/shard_map/ppermute | solution.py:32
  157.0 1.0 dynamic-slice_bitcast_fusion.4
  158.0 1.1 collective-permute-start.26
  159.1 1.5 collective-permute-start.27
  160.7 2.5 %collective-permute-done.29 = bf16[5376,128]{1,0:T(8,128)(2,1)S(1)} collective-permute-done((bf16[5376,128]{1,0:T(8,128)(2,1)S(1)}, bf16[5376,128]{1,0:T(8,128)(2,1)S(1)}, u32[]{:S(2)}, u32[]{:S(2)}) %collective-permute-start.29) | collective-permute-done | bytes 1376288 | tf_op jit(solution)/shard_map/ppermute | solution.py:32
  163.2 1.8 collective-permute-start.28
  165.4 1.1 dynamic-slice_bitcast_fusion
  166.5 1.5 collective-permute-start.30
  168.4 1.6 collective-permute-start.31
  170.0 1.5 copy-done.6
  171.8 1.3 copy-done.3
  173.1 1.3 copy-done.5
  174.4 1.8 copy-done.7
  176.2 1.3 copy-done.9
  177.6 1.3 copy-done.11
  178.9 5.9 %token_terms.1 = bf16[256,5376]{1,0:T(8,128)(2,1)} custom-call(bf16[256,512]{1,0:T(8,128)(2,1)S(1)} %get-tuple-element.90.own_ref, bf16[256,512]{1,0:T(8,128)(2,1)S(1)} %collective-permute-done.20.far_ref, bf16[5376,128]{1,0:T(8,128)(2,1)S(1)} %bitcast.92, bf16[5376,128]{1,0:T(8,128)(2,1)S(1)} %copy-done.9, bf16[5376,128]{1,0:T(8,128)(2,1)S(1)} %bitcast.89, ...), custom_call_target="tpu_custom_call" | custom-call | tf_op jit(solution)/shard_map/token_terms/pallas_call | solution.py:166
  184.8 4.7 %all-to-all-start = ((bf16[4,64,5376]{2,1,0:T(8,128)(2,1)}), bf16[4,64,5376]{2,1,0:T(8,128)(2,1)}, u32[]{:S(2)}, u32[]{:S(2)}) async-start(bf16[4,64,5376]{2,1,0:T(8,128)(2,1)} %bitcast.24), calls=%async_computation | async-start | bytes 5505024 | tf_op jit(solution)/shard_map/all_to_all | solution.py:366
  189.6 2.3 %collective-permute-done.32 = bf16[1344,128]{1,0:T(8,128)(2,1)} collective-permute-done((bf16[1344,128]{1,0:T(8,128)(2,1)}, bf16[1344,128]{1,0:T(8,128)(2,1)}, u32[]{:S(2)}, u32[]{:S(2)}) %collective-permute-start.32) | collective-permute-done | bytes 344096 | tf_op jit(solution)/shard_map/ppermute | solution.py:32
  191.9 1.3 add_convert_fusion.3
  193.2 1.4 add_convert_fusion.4
  194.8 5.1 %collective-permute-start.34 = (bf16[336,256]{1,0:T(8,128)(2,1)S(1)}, bf16[336,256]{1,0:T(8,128)(2,1)S(1)}, u32[]{:S(2)}, u32[]{:S(2)}) collective-permute-start(bf16[336,256]{1,0:T(8,128)(2,1)S(1)} %get-tuple-element.86), channel_id=1, source_target_pairs={{0,48},{8,56},{16,0},{24,8},{32,16},{40,24},{48,32},{56,40},{64,11... | collective-permute-start | bytes 516104 | tf_op jit(solution)/shard_map/ppermute | solution.py:32
  200.5 2.9 %collective-permute-done.34 = bf16[336,256]{1,0:T(8,128)(2,1)S(1)} collective-permute-done((bf16[336,256]{1,0:T(8,128)(2,1)S(1)}, bf16[336,256]{1,0:T(8,128)(2,1)S(1)}, u32[]{:S(2)}, u32[]{:S(2)}) %collective-permute-start.34) | collective-permute-done | bytes 172064 | tf_op jit(solution)/shard_map/ppermute | solution.py:32
  203.4 7.4 %collective-permute-done.33 = bf16[336,256]{1,0:T(8,128)(2,1)S(1)} collective-permute-done((bf16[336,256]{1,0:T(8,128)(2,1)S(1)}, bf16[336,256]{1,0:T(8,128)(2,1)S(1)}, u32[]{:S(2)}, u32[]{:S(2)}) %collective-permute-start.33) | collective-permute-done | bytes 172064 | tf_op jit(solution)/shard_map/ppermute | solution.py:32
  210.9 2.0 collective-permute-start.36
  214.2 1.9 adam_step.1
  216.1 4.4 %all-to-all-done = bf16[4,64,5376]{2,1,0:T(8,128)(2,1)} async-done(((bf16[4,64,5376]{2,1,0:T(8,128)(2,1)}), bf16[4,64,5376]{2,1,0:T(8,128)(2,1)}, u32[]{:S(2)}, u32[]{:S(2)}) %all-to-all-start) | async-done | bytes 2752544 | tf_op jit(solution)/shard_map/all_to_all | solution.py:366
  220.5 2.9 %fusion.14 = bf16[64,5376]{1,0:T(8,128)(2,1)} fusion(bf16[4,64,5376]{2,1,0:T(8,128)(2,1)} %all-to-all-done), kind=kLoop, calls=%fused_computation.13 | loop fusion | flops 2752512 | bytes 3440640 | tf_op jit(solution)/shard_map/add | solution.py:83
  (125 shorter events, 10.5 us)
Async XLA Ops:
  2.0 4.2 %collective-permute-start = (bf16[168,256]{1,0:T(8,128)(2,1)S(1)}, bf16[168,256]{1,0:T(8,128)(2,1)S(1)}, u32[]{:S(2)}, u32[]{:S(2)}) collective-permute-start(bf16[168,256]{1,0:T(8,128)(2,1)S(1)} %pad_maximum_fusion.5), channel_id=1, source_target_pairs={{0,8},{8,0},{16,24},{24,16},{32,40},{40,32},{48,56},{56,48},{64,72... | collective-permute-start | bytes 258056 | tf_op jit(solution)/shard_map/ppermute | solution.py:32
  6.3 7.5 %collective-permute-start.1 = (bf16[336,256]{1,0:T(8,128)(2,1)S(1)}, bf16[336,256]{1,0:T(8,128)(2,1)S(1)}, u32[]{:S(2)}, u32[]{:S(2)}) collective-permute-start(bf16[336,256]{1,0:T(8,128)(2,1)S(1)} %pad_maximum_fusion.4), channel_id=1, source_target_pairs={{0,16},{8,24},{16,32},{24,40},{32,48},{40,56},{48,0},{56,8},{64,80... | collective-permute-start | bytes 516104 | tf_op jit(solution)/shard_map/ppermute | solution.py:32
  6.5 14.7 %collective-permute-start.2 = (bf16[336,256]{1,0:T(8,128)(2,1)S(1)}, bf16[336,256]{1,0:T(8,128)(2,1)S(1)}, u32[]{:S(2)}, u32[]{:S(2)}) collective-permute-start(bf16[336,256]{1,0:T(8,128)(2,1)S(1)} %pad_maximum_fusion.4), channel_id=1, source_target_pairs={{0,32},{8,40},{16,48},{24,56},{32,0},{40,8},{48,16},{56,24},{64,96... | collective-permute-start | bytes 516104 | tf_op jit(solution)/shard_map/ppermute | solution.py:32
  9.3 11.9 %collective-permute-start.3 = (bf16[336,256]{1,0:T(8,128)(2,1)S(1)}, bf16[336,256]{1,0:T(8,128)(2,1)S(1)}, u32[]{:S(2)}, u32[]{:S(2)}) collective-permute-start(bf16[336,256]{1,0:T(8,128)(2,1)S(1)} %pad_maximum_fusion.4), channel_id=1, source_target_pairs={{0,48},{8,56},{16,0},{24,8},{32,16},{40,24},{48,32},{56,40},{64,11... | collective-permute-start | bytes 516104 | tf_op jit(solution)/shard_map/ppermute | solution.py:32
  21.3 9.6 %collective-permute-start.4 = (bf16[1344,128]{1,0:T(8,128)(2,1)S(1)}, bf16[1344,128]{1,0:T(8,128)(2,1)S(1)}, u32[]{:S(2)}, u32[]{:S(2)}) collective-permute-start(bf16[1344,128]{1,0:T(8,128)(2,1)S(1)} %get-tuple-element.87), channel_id=1, source_target_pairs={{0,64},{8,72},{16,80},{24,88},{32,96},{40,104},{48,112},{56,120},{... | collective-permute-start | bytes 1032200 | tf_op jit(solution)/shard_map/ppermute | solution.py:32
  22.6 8.8 %collective-permute-start.5 = (bf16[1344,128]{1,0:T(8,128)(2,1)S(1)}, bf16[1344,128]{1,0:T(8,128)(2,1)S(1)}, u32[]{:S(2)}, u32[]{:S(2)}) collective-permute-start(bf16[1344,128]{1,0:T(8,128)(2,1)S(1)} %get-tuple-element.87), channel_id=1, source_target_pairs={{0,192},{8,200},{16,208},{24,216},{32,224},{40,232},{48,240},{56,2... | collective-permute-start | bytes 1032200 | tf_op jit(solution)/shard_map/ppermute | solution.py:32
  24.1 16.0 %collective-permute-start.6 = (bf16[1344,128]{1,0:T(8,128)(2,1)S(1)}, bf16[1344,128]{1,0:T(8,128)(2,1)S(1)}, u32[]{:S(2)}, u32[]{:S(2)}) collective-permute-start(bf16[1344,128]{1,0:T(8,128)(2,1)S(1)} %get-tuple-element.87), channel_id=1, source_target_pairs={{0,128},{8,136},{16,144},{24,152},{32,160},{40,168},{48,176},{56,1... | collective-permute-start | bytes 1032200 | tf_op jit(solution)/shard_map/ppermute | solution.py:32
  40.1 59.0 %slice-start = ((s8[5505024]{0:T(1024)(128)(4,1)}), s8[4194304]{0:T(1024)(128)(4,1)S(1)}, s32[]{:S(2)}) async-start(s8[5505024]{0:T(1024)(128)(4,1)} %bitcast.83), calls=%async_computation.1 | async-start | bytes 8388608
  40.1 9.1 %copy-start.4 = (bf16[4,1344,128]{2,1,0:T(8,128)(2,1)}, bf16[4,1344,128]{2,1,0:T(8,128)(2,1)S(1)}, u32[]{:S(2)}) copy-start(bf16[4,1344,128]{2,1,0:T(8,128)(2,1)S(1)} %bitcast_dynamic-update-slice_fusion.6) | copy-start | bytes 4128772
  40.1 4.4 %collective-permute-start.7 = (bf16[5376,128]{1,0:T(8,128)(2,1)S(1)}, bf16[5376,128]{1,0:T(8,128)(2,1)S(1)}, u32[]{:S(2)}, u32[]{:S(2)}) collective-permute-start(bf16[5376,128]{1,0:T(8,128)(2,1)S(1)} %bitcast.90), channel_id=1, source_target_pairs={{0,8},{8,0},{16,24},{24,16},{32,40},{40,32},{48,56},{56,48},{64,72... | collective-permute-start | bytes 4128776 | tf_op jit(solution)/shard_map/ppermute | solution.py:32
  41.6 57.5 %slice-start.1 = ((s8[5505024]{0:T(1024)(128)(4,1)}), s8[1310720]{0:T(1024)(128)(4,1)S(1)}, s32[]{:S(2)}) async-start(s8[5505024]{0:T(1024)(128)(4,1)} %bitcast.83), calls=%async_computation.2 | async-start | bytes 2621440
  41.6 10.7 %collective-permute-start.8 = (bf16[1344,128]{1,0:T(8,128)(2,1)S(1)}, bf16[1344,128]{1,0:T(8,128)(2,1)S(1)}, u32[]{:S(2)}, u32[]{:S(2)}) collective-permute-start(bf16[1344,128]{1,0:T(8,128)(2,1)S(1)} %get-tuple-element.36), channel_id=1, source_target_pairs={{0,64},{8,72},{16,80},{24,88},{32,96},{40,104},{48,112},{56,120},{... | collective-permute-start | bytes 1032200 | tf_op jit(solution)/shard_map/ppermute | solution.py:32
  42.5 9.9 %collective-permute-start.9 = (bf16[1344,128]{1,0:T(8,128)(2,1)S(1)}, bf16[1344,128]{1,0:T(8,128)(2,1)S(1)}, u32[]{:S(2)}, u32[]{:S(2)}) collective-permute-start(bf16[1344,128]{1,0:T(8,128)(2,1)S(1)} %get-tuple-element.36), channel_id=1, source_target_pairs={{0,192},{8,200},{16,208},{24,216},{32,224},{40,232},{48,240},{56,2... | collective-permute-start | bytes 1032200 | tf_op jit(solution)/shard_map/ppermute | solution.py:32
  44.3 15.7 %collective-permute-start.10 = (bf16[1344,128]{1,0:T(8,128)(2,1)S(1)}, bf16[1344,128]{1,0:T(8,128)(2,1)S(1)}, u32[]{:S(2)}, u32[]{:S(2)}) collective-permute-start(bf16[1344,128]{1,0:T(8,128)(2,1)S(1)} %get-tuple-element.36), channel_id=1, source_target_pairs={{0,128},{8,136},{16,144},{24,152},{32,160},{40,168},{48,176},{56,1... | collective-permute-start | bytes 1032200 | tf_op jit(solution)/shard_map/ppermute | solution.py:32
  44.5 4.7 %copy-start.8 = (bf16[5376,128]{1,0:T(8,128)(2,1)}, bf16[5376,128]{1,0:T(8,128)(2,1)S(1)}, u32[]{:S(2)}) copy-start(bf16[5376,128]{1,0:T(8,128)(2,1)S(1)} %collective-permute-done.7.kb_ref) | copy-start | bytes 4128772
  60.3 40.4 %copy-start.2 = (bf16[4,1344,128]{2,1,0:T(8,128)(2,1)}, bf16[4,1344,128]{2,1,0:T(8,128)(2,1)S(1)}, u32[]{:S(2)}) copy-start(bf16[4,1344,128]{2,1,0:T(8,128)(2,1)S(1)} %bitcast_dynamic-update-slice_fusion.3) | copy-start | bytes 4128772
  60.3 38.8 %collective-permute-start.11 = (bf16[5376,128]{1,0:T(8,128)(2,1)S(1)}, bf16[5376,128]{1,0:T(8,128)(2,1)S(1)}, u32[]{:S(2)}, u32[]{:S(2)}) collective-permute-start(bf16[5376,128]{1,0:T(8,128)(2,1)S(1)} %bitcast.87), channel_id=1, source_target_pairs={{0,8},{8,0},{16,24},{24,16},{32,40},{40,32},{48,56},{56,48},{64,72... | collective-permute-start | bytes 4128776 | tf_op jit(solution)/shard_map/ppermute | solution.py:32
  61.4 10.1 %collective-permute-start.12 = (bf16[336,256]{1,0:T(8,128)(2,1)S(1)}, bf16[336,256]{1,0:T(8,128)(2,1)S(1)}, u32[]{:S(2)}, u32[]{:S(2)}) collective-permute-start(bf16[336,256]{1,0:T(8,128)(2,1)S(1)} %pad_maximum_fusion.4), channel_id=1, source_target_pairs={{0,4},{1,5},{2,6},{3,7},{4,0},{5,1},{6,2},{7,3},{8,12},{9,13},{10,... | collective-permute-start | bytes 516104 | tf_op jit(solution)/shard_map/ppermute | solution.py:40
  71.5 11.0 %collective-permute-start.13 = (bf16[336,256]{1,0:T(8,128)(2,1)S(1)}, bf16[336,256]{1,0:T(8,128)(2,1)S(1)}, u32[]{:S(2)}, u32[]{:S(2)}) collective-permute-start(bf16[336,256]{1,0:T(8,128)(2,1)S(1)} %collective-permute-done.12), channel_id=1, source_target_pairs={{0,16},{8,24},{16,32},{24,40},{32,48},{40,56},{48,0},{56,8},{64,80... | collective-permute-start | bytes 516104 | tf_op jit(solution)/shard_map/ppermute | solution.py:32
  80.0 10.8 %collective-permute-start.14 = (bf16[336,256]{1,0:T(8,128)(2,1)S(1)}, bf16[336,256]{1,0:T(8,128)(2,1)S(1)}, u32[]{:S(2)}, u32[]{:S(2)}) collective-permute-start(bf16[336,256]{1,0:T(8,128)(2,1)S(1)} %collective-permute-done.12), channel_id=1, source_target_pairs={{0,32},{8,40},{16,48},{24,56},{32,0},{40,8},{48,16},{56,24},{64,96... | collective-permute-start | bytes 516104 | tf_op jit(solution)/shard_map/ppermute | solution.py:32
  80.2 10.6 %collective-permute-start.15 = (bf16[336,256]{1,0:T(8,128)(2,1)S(1)}, bf16[336,256]{1,0:T(8,128)(2,1)S(1)}, u32[]{:S(2)}, u32[]{:S(2)}) collective-permute-start(bf16[336,256]{1,0:T(8,128)(2,1)S(1)} %collective-permute-done.12), channel_id=1, source_target_pairs={{0,48},{8,56},{16,0},{24,8},{32,16},{40,24},{48,32},{56,40},{64,11... | collective-permute-start | bytes 516104 | tf_op jit(solution)/shard_map/ppermute | solution.py:32
  90.9 32.9 %copy-start.16 = (bf16[4,336,256]{2,1,0:T(8,128)(2,1)}, bf16[4,336,256]{2,1,0:T(8,128)(2,1)S(1)}, u32[]{:S(2)}) copy-start(bf16[4,336,256]{2,1,0:T(8,128)(2,1)S(1)} %bitcast_dynamic-update-slice_fusion.9) | copy-start | bytes 2064388
  90.9 11.0 %collective-permute-start.16 = (bf16[512,256]{1,0:T(8,128)(2,1)S(1)}, bf16[512,256]{1,0:T(8,128)(2,1)S(1)}, u32[]{:S(2)}, u32[]{:S(2)}) collective-permute-start(bf16[512,256]{1,0:T(8,128)(2,1)S(1)} %pad_maximum_fusion.2.own_ref), channel_id=1, source_target_pairs={{0,16},{8,24},{16,32},{24,40},{32,48},{40,56},{48,64},{56,72},{64,... | collective-permute-start | bytes 786440 | tf_op jit(solution)/shard_map/ppermute | solution.py:49
  96.8 8.9 %collective-permute-start.17 = (bf16[512,256]{1,0:T(8,128)(2,1)S(1)}, bf16[512,256]{1,0:T(8,128)(2,1)S(1)}, u32[]{:S(2)}, u32[]{:S(2)}) collective-permute-start(bf16[512,256]{1,0:T(8,128)(2,1)S(1)} %pad_maximum_fusion.2.own_ref), channel_id=1, source_target_pairs={{0,8},{8,16},{16,24},{24,32},{32,40},{40,48},{48,56},{56,64},{64,7... | collective-permute-start | bytes 786440 | tf_op jit(solution)/shard_map/ppermute | solution.py:49
  99.1 6.6 %copy-start.15 = (bf16[512,256]{1,0:T(8,128)(2,1)S(1)}, bf16[512,256]{1,0:T(8,128)(2,1)}, u32[]{:S(2)}) copy-start(bf16[512,256]{1,0:T(8,128)(2,1)} %cot_ref.1) | copy-start | bytes 786436
  99.1 1.6 copy-start.10
  113.9 18.3 %collective-permute-start.19 = (bf16[512,256]{1,0:T(8,128)(2,1)S(1)}, bf16[512,256]{1,0:T(8,128)(2,1)S(1)}, u32[]{:S(2)}, u32[]{:S(2)}) collective-permute-start(bf16[512,256]{1,0:T(8,128)(2,1)S(1)} %get-tuple-element.47), channel_id=1, source_target_pairs={{16,0},{24,8},{32,16},{40,24},{48,32},{56,40},{64,48},{72,56},{80,... | collective-permute-start | bytes 786440 | tf_op jit(solution)/shard_map/ppermute | solution.py:49
  115.2 18.0 %collective-permute-start.18 = (bf16[512,256]{1,0:T(8,128)(2,1)S(1)}, bf16[512,256]{1,0:T(8,128)(2,1)S(1)}, u32[]{:S(2)}, u32[]{:S(2)}) collective-permute-start(bf16[512,256]{1,0:T(8,128)(2,1)S(1)} %get-tuple-element.46), channel_id=1, source_target_pairs={{8,0},{16,8},{24,16},{32,24},{40,32},{48,40},{56,48},{64,56},{72,6... | collective-permute-start | bytes 786440 | tf_op jit(solution)/shard_map/ppermute | solution.py:49
  117.1 27.6 %collective-permute-start.21 = (bf16[1344,256]{1,0:T(8,128)(2,1)S(1)}, bf16[1344,256]{1,0:T(8,128)(2,1)S(1)}, u32[]{:S(2)}, u32[]{:S(2)}) collective-permute-start(bf16[1344,256]{1,0:T(8,128)(2,1)S(1)} %bitcast.100), channel_id=1, source_target_pairs={{0,64},{8,72},{16,80},{24,88},{32,96},{40,104},{48,112},{56,120},{... | collective-permute-start | bytes 2064392 | tf_op jit(solution)/shard_map/ppermute | solution.py:32
  123.8 21.0 %collective-permute-start.22 = (bf16[1344,256]{1,0:T(8,128)(2,1)S(1)}, bf16[1344,256]{1,0:T(8,128)(2,1)S(1)}, u32[]{:S(2)}, u32[]{:S(2)}) collective-permute-start(bf16[1344,256]{1,0:T(8,128)(2,1)S(1)} %bitcast.101), channel_id=1, source_target_pairs={{0,192},{8,200},{16,208},{24,216},{32,224},{40,232},{48,240},{56,2... | collective-permute-start | bytes 2064392 | tf_op jit(solution)/shard_map/ppermute | solution.py:32
  123.8 31.7 %collective-permute-start.23 = (bf16[1344,256]{1,0:T(8,128)(2,1)S(1)}, bf16[1344,256]{1,0:T(8,128)(2,1)S(1)}, u32[]{:S(2)}, u32[]{:S(2)}) collective-permute-start(bf16[1344,256]{1,0:T(8,128)(2,1)S(1)} %bitcast.102), channel_id=1, source_target_pairs={{0,128},{8,136},{16,144},{24,152},{32,160},{40,168},{48,176},{56,1... | collective-permute-start | bytes 2064392 | tf_op jit(solution)/shard_map/ppermute | solution.py:32
  126.4 2.6 %copy-start = (bf16[512,5376]{1,0:T(8,128)(2,1)S(1)}, bf16[512,5376]{1,0:T(8,128)(2,1)}, u32[]{:S(2)}) copy-start(bf16[512,5376]{1,0:T(8,128)(2,1)} %n_ref.3) | copy-start | bytes 16515076
  132.2 24.4 %collective-permute-start.25 = (bf16[5376,128]{1,0:T(8,128)(2,1)S(1)}, bf16[5376,128]{1,0:T(8,128)(2,1)S(1)}, u32[]{:S(2)}, u32[]{:S(2)}) collective-permute-start(bf16[5376,128]{1,0:T(8,128)(2,1)S(1)} %get-tuple-element.53), channel_id=1, source_target_pairs={{0,8},{8,0},{16,24},{24,16},{32,40},{40,32},{48,56},{56,48},{64,72... | collective-permute-start | bytes 4128776 | tf_op jit(solution)/shard_map/ppermute | solution.py:32
  133.7 32.8 %collective-permute-start.20 = (bf16[256,512]{1,0:T(8,128)(2,1)S(1)}, bf16[256,512]{1,0:T(8,128)(2,1)S(1)}, u32[]{:S(2)}, u32[]{:S(2)}) collective-permute-start(bf16[256,512]{1,0:T(8,128)(2,1)S(1)} %get-tuple-element.89), channel_id=1, source_target_pairs={{0,4},{1,5},{2,6},{3,7},{4,0},{5,1},{6,2},{7,3},{8,12},{9,13},{10,... | collective-permute-start | bytes 786440 | tf_op jit(solution)/shard_map/ppermute | solution.py:40
  139.0 2.6 %copy-start.1 = (bf16[512,5376]{1,0:T(8,128)(2,1)S(1)}, bf16[512,5376]{1,0:T(8,128)(2,1)}, u32[]{:S(2)}) copy-start(bf16[512,5376]{1,0:T(8,128)(2,1)} %n_ref.3) | copy-start | bytes 16515076
  141.6 13.9 %copy-start.17 = (bf16[4,336,256]{2,1,0:T(8,128)(2,1)S(1)}, bf16[4,336,256]{2,1,0:T(8,128)(2,1)}, u32[]{:S(2)}) copy-start(bf16[4,336,256]{2,1,0:T(8,128)(2,1)} %copy-done.16) | copy-start | bytes 2064388
  155.9 14.1 %collective-permute-start.24 = (bf16[5376,256]{1,0:T(8,128)(2,1)S(1)}, bf16[5376,256]{1,0:T(8,128)(2,1)S(1)}, u32[]{:S(2)}, u32[]{:S(2)}) collective-permute-start(bf16[5376,256]{1,0:T(8,128)(2,1)S(1)} %bitcast.85), channel_id=1, source_target_pairs={{0,8},{8,0},{16,24},{24,16},{32,40},{40,32},{48,56},{56,48},{64,72... | collective-permute-start | bytes 8257544 | tf_op jit(solution)/shard_map/ppermute | solution.py:32
  156.5 6.7 %collective-permute-start.29 = (bf16[5376,128]{1,0:T(8,128)(2,1)S(1)}, bf16[5376,128]{1,0:T(8,128)(2,1)S(1)}, u32[]{:S(2)}, u32[]{:S(2)}) collective-permute-start(bf16[5376,128]{1,0:T(8,128)(2,1)S(1)} %get-tuple-element.55), channel_id=1, source_target_pairs={{0,8},{8,0},{16,24},{24,16},{32,40},{40,32},{48,56},{56,48},{64,72... | collective-permute-start | bytes 4128776 | tf_op jit(solution)/shard_map/ppermute | solution.py:32
  158.0 10.4 %collective-permute-start.26 = (bf16[1344,128]{1,0:T(8,128)(2,1)S(1)}, bf16[1344,128]{1,0:T(8,128)(2,1)S(1)}, u32[]{:S(2)}, u32[]{:S(2)}) collective-permute-start(bf16[1344,128]{1,0:T(8,128)(2,1)S(1)} %get-tuple-element.82), channel_id=1, source_target_pairs={{0,64},{8,72},{16,80},{24,88},{32,96},{40,104},{48,112},{56,120},{... | collective-permute-start | bytes 1032200 | tf_op jit(solution)/shard_map/ppermute | solution.py:32
  159.1 30.4 %collective-permute-start.27 = (bf16[1344,128]{1,0:T(8,128)(2,1)}, bf16[1344,128]{1,0:T(8,128)(2,1)}, u32[]{:S(2)}, u32[]{:S(2)}) collective-permute-start(bf16[1344,128]{1,0:T(8,128)(2,1)} %get-tuple-element.81), channel_id=1, source_target_pairs={{0,192},{8,200},{16,208},{24,216},{32,224},{40,232},{48,240},{56,2... | collective-permute-start | bytes 1032200 | tf_op jit(solution)/shard_map/ppermute | solution.py:32
  163.2 26.3 %collective-permute-start.28 = (bf16[1344,128]{1,0:T(8,128)(2,1)}, bf16[1344,128]{1,0:T(8,128)(2,1)}, u32[]{:S(2)}, u32[]{:S(2)}) collective-permute-start(bf16[1344,128]{1,0:T(8,128)(2,1)} %get-tuple-element.80), channel_id=1, source_target_pairs={{0,128},{8,136},{16,144},{24,152},{32,160},{40,168},{48,176},{56,1... | collective-permute-start | bytes 1032200 | tf_op jit(solution)/shard_map/ppermute | solution.py:32
  166.5 23.1 %collective-permute-start.30 = (bf16[1344,128]{1,0:T(8,128)(2,1)}, bf16[1344,128]{1,0:T(8,128)(2,1)}, u32[]{:S(2)}, u32[]{:S(2)}) collective-permute-start(bf16[1344,128]{1,0:T(8,128)(2,1)} %get-tuple-element.78), channel_id=1, source_target_pairs={{0,64},{8,72},{16,80},{24,88},{32,96},{40,104},{48,112},{56,120},{... | collective-permute-start | bytes 1032200 | tf_op jit(solution)/shard_map/ppermute | solution.py:32
  168.4 1.6 copy-start.20
  168.4 21.2 %collective-permute-start.31 = (bf16[1344,128]{1,0:T(8,128)(2,1)}, bf16[1344,128]{1,0:T(8,128)(2,1)}, u32[]{:S(2)}, u32[]{:S(2)}) collective-permute-start(bf16[1344,128]{1,0:T(8,128)(2,1)} %get-tuple-element.77), channel_id=1, source_target_pairs={{0,192},{8,200},{16,208},{24,216},{32,224},{40,232},{48,240},{56,2... | collective-permute-start | bytes 1032200 | tf_op jit(solution)/shard_map/ppermute | solution.py:32
  170.0 1.5 copy-start.6
  171.5 20.4 %collective-permute-start.32 = (bf16[1344,128]{1,0:T(8,128)(2,1)}, bf16[1344,128]{1,0:T(8,128)(2,1)}, u32[]{:S(2)}, u32[]{:S(2)}) collective-permute-start(bf16[1344,128]{1,0:T(8,128)(2,1)} %get-tuple-element.76), channel_id=1, source_target_pairs={{0,128},{8,136},{16,144},{24,152},{32,160},{40,168},{48,176},{56,1... | collective-permute-start | bytes 1032200 | tf_op jit(solution)/shard_map/ppermute | solution.py:32
  171.8 1.3 copy-start.3
  173.1 1.3 copy-start.5
  174.4 1.8 copy-start.7
  176.2 1.3 copy-start.9
  177.6 1.3 copy-start.11
  184.8 7.1 %copy-start.18 = (bf16[1344,128]{1,0:T(8,128)(2,1)S(1)}, bf16[1344,128]{1,0:T(8,128)(2,1)}, u32[]{:S(2)}) copy-start(bf16[1344,128]{1,0:T(8,128)(2,1)} %get-tuple-element.63) | copy-start | bytes 1032196
  184.8 7.1 %copy-start.21 = (bf16[1344,128]{1,0:T(8,128)(2,1)S(1)}, bf16[1344,128]{1,0:T(8,128)(2,1)}, u32[]{:S(2)}) copy-start(bf16[1344,128]{1,0:T(8,128)(2,1)} %copy-done.20) | copy-start | bytes 1032196
  184.8 35.6 %all-to-all-start = ((bf16[4,64,5376]{2,1,0:T(8,128)(2,1)}), bf16[4,64,5376]{2,1,0:T(8,128)(2,1)}, u32[]{:S(2)}, u32[]{:S(2)}) async-start(bf16[4,64,5376]{2,1,0:T(8,128)(2,1)} %bitcast.24), calls=%async_computation | async-start | bytes 5505024 | tf_op jit(solution)/shard_map/all_to_all | solution.py:366
  189.6 3.6 %copy-start.19 = (bf16[1344,128]{1,0:T(8,128)(2,1)S(1)}, bf16[1344,128]{1,0:T(8,128)(2,1)}, u32[]{:S(2)}) copy-start(bf16[1344,128]{1,0:T(8,128)(2,1)} %get-tuple-element.59) | copy-start | bytes 1032196
  194.6 18.3 %copy-start.22 = (s32[8]{0:T(128)S(1)}, s32[8]{0:T(128)}, u32[]{:S(2)}) copy-start(s32[8]{0:T(128)} %param.12) | copy-start | bytes 100
  194.6 19.6 %copy-start.12 = (f32[168,1,512]{2,1,0:T(1,128)S(1)}, f32[168,1,512]{2,1,0:T(1,128)}, u32[]{:S(2)}) copy-start(f32[168,1,512]{2,1,0:T(1,128)} %param.9) | copy-start | bytes 1032196
  194.6 19.6 %copy-start.13 = (f32[168,1,512]{2,1,0:T(1,128)S(1)}, f32[168,1,512]{2,1,0:T(1,128)}, u32[]{:S(2)}) copy-start(f32[168,1,512]{2,1,0:T(1,128)} %param.10) | copy-start | bytes 1032196
  194.7 19.6 %copy-start.14 = (f32[168,1,512]{2,1,0:T(1,128)S(1)}, f32[168,1,512]{2,1,0:T(1,128)}, u32[]{:S(2)}) copy-start(f32[168,1,512]{2,1,0:T(1,128)} %param.11) | copy-start | bytes 1032196
  194.7 5.8 %collective-permute-start.35 = (bf16[336,256]{1,0:T(8,128)(2,1)S(1)}, bf16[336,256]{1,0:T(8,128)(2,1)S(1)}, u32[]{:S(2)}, u32[]{:S(2)}) collective-permute-start(bf16[336,256]{1,0:T(8,128)(2,1)S(1)} %get-tuple-element.85), channel_id=1, source_target_pairs={{0,32},{8,40},{16,48},{24,56},{32,0},{40,8},{48,16},{56,24},{64,96... | collective-permute-start | bytes 516104 | tf_op jit(solution)/shard_map/ppermute | solution.py:32
  194.8 8.6 %collective-permute-start.34 = (bf16[336,256]{1,0:T(8,128)(2,1)S(1)}, bf16[336,256]{1,0:T(8,128)(2,1)S(1)}, u32[]{:S(2)}, u32[]{:S(2)}) collective-permute-start(bf16[336,256]{1,0:T(8,128)(2,1)S(1)} %get-tuple-element.86), channel_id=1, source_target_pairs={{0,48},{8,56},{16,0},{24,8},{32,16},{40,24},{48,32},{56,40},{64,11... | collective-permute-start | bytes 516104 | tf_op jit(solution)/shard_map/ppermute | solution.py:32
  199.9 10.9 %collective-permute-start.33 = (bf16[336,256]{1,0:T(8,128)(2,1)S(1)}, bf16[336,256]{1,0:T(8,128)(2,1)S(1)}, u32[]{:S(2)}, u32[]{:S(2)}) collective-permute-start(bf16[336,256]{1,0:T(8,128)(2,1)S(1)} %get-tuple-element.84), channel_id=1, source_target_pairs={{0,16},{8,24},{16,32},{24,40},{32,48},{40,56},{48,0},{56,8},{64,80... | collective-permute-start | bytes 516104 | tf_op jit(solution)/shard_map/ppermute | solution.py:32
  210.9 3.3 %collective-permute-start.36 = (f32[168,256]{1,0:T(8,128)S(1)}, f32[168,256]{1,0:T(8,128)S(1)}, u32[]{:S(2)}, u32[]{:S(2)}) collective-permute-start(f32[168,256]{1,0:T(8,128)S(1)} %get-tuple-element.91), channel_id=1, source_target_pairs={{0,8},{8,0},{16,24},{24,16},{32,40},{40,32},{48,56},{56,48},{64,72... | collective-permute-start | bytes 516104 | tf_op jit(solution)/shard_map/ppermute | solution.py:32
where the time goes:
time: 228 us; the launch traced here: 223 us
  waiting for transfers between devices  85.5 us (38%)
  starting transfers between devices  79.8 us (35%)
  Pallas kernels  22.4 us (10%)
  local copies, waits for them, and re-layouts  17.9 us (8%)
  other arithmetic  9.45 us (4%)
  matrix products  6.23 us (3%)
    ppermute x31, waiting for transfers between devices, seq_move(): return lax.ppermute(block, 'seq', pairs)  71.6 us
    ppermute x31, starting transfers between devices, seq_move(): return lax.ppermute(block, 'seq', pairs)  52.9 us
    unnamed x51, local copies, waits for them, and re-layouts  13.8 us
    ppermute x4, starting transfers between devices, shifted(): return lax.ppermute(block, 'seq', route)  11.3 us
    ppermute x2, starting transfers between devices, head_move(): return lax.ppermute(block, 'head', pairs)  10.8 us
    pallas_call x1, Pallas kernels, attend(): pl.pallas_call(attend_kernel, grid_spec=pltpu.PrefetchScalarGridSpec(num_...  8.19 us
    pallas_call x2, Pallas kernels, weight_terms(): pl.pallas_call(term_kernel, in_specs=[near(), near()], out_specs=[near(),...  6.4 us
    pallas_call x1, Pallas kernels, token_terms(): pl.pallas_call(tokens_kernel, in_specs=[near()] * 8, out_specs=near(), ou...  5.93 us
  transfers between devices with their start and end apart: 38, of which 21 were waited for; matrix products, arithmetic and copies ran while one was open for 7% of the time, Pallas kernels for 6%

commit v1 on v0

--- a/solution.py
+++ b/solution.py
@@ -116,19 +116,35 @@
     return pl.BlockSpec(memory_space=pltpu.VMEM)
 
 
+def far_off():
+    return pl.BlockSpec(memory_space=pltpu.HBM)
+
+
 def limit(mib):
     return pltpu.CompilerParams(vmem_limit_bytes=mib << 20)
 
 
-def term_kernel(n_ref, g_ref, keep_ref, send_ref, turned):
+def term_kernel(n_ref, g_ref, keep_ref, send_ref, turned, held, sems):
+    tiles = n_ref.shape[1] // TILE
+
+    def tile(i):
+        return pl.ds(pl.multiple_of(i * TILE, TILE), TILE)
+
+    def copy(i):
+        return pltpu.make_async_copy(n_ref.at[:, tile(i)], held.at[:, tile(i)], sems.at[i])
+
+    @pl.loop(0, tiles)
+    def _(i):
+        copy(i).start()
+
     turned[...] = g_ref[...].T
 
-    @pl.loop(0, n_ref.shape[1] // TILE)
+    @pl.loop(0, tiles)
     def _(i):
-        spot = pl.ds(pl.multiple_of(i * TILE, TILE), TILE)
-        out = jnp.dot(turned[...], n_ref[:, spot], preferred_element_type=f32).astype(bf16).T
-        keep_ref[spot, :] = out[:, :HEAD_DIM]
-        send_ref[spot, :] = out[:, HEAD_DIM:]
+        copy(i).wait()
+        out = jnp.dot(turned[...], held[:, tile(i)], preferred_element_type=f32).astype(bf16).T
+        keep_ref[tile(i), :] = out[:, :HEAD_DIM]
+        send_ref[tile(i), :] = out[:, HEAD_DIM:]
 
 
 def weight_terms(normed, pair):
@@ -136,28 +152,51 @@
     shape = jax.ShapeDtypeStruct((width, HEAD_DIM), bf16)
     return pl.pallas_call(
         term_kernel,
-        in_specs=[near(), near()],
+        in_specs=[far_off(), near()],
         out_specs=[near(), near()],
         out_shape=[shape, shape],
-        scratch_shapes=[pltpu.VMEM((2 * HEAD_DIM, rows), bf16)],
-        compiler_params=limit(8),
+        scratch_shapes=[
+            pltpu.VMEM((2 * HEAD_DIM, rows), bf16),
+            pltpu.VMEM((rows, width), bf16),
+            pltpu.SemaphoreType.DMA((width // TILE,)),
+        ],
+        compiler_params=limit(50),
         name="weight_terms",
     )(normed, pair)
 
 
-def tokens_kernel(own_ref, far_ref, ka_ref, kb_ref, qa_ref, qb_ref, fa_ref, fb_ref, o_ref, turned):
+def tokens_kernel(own_ref, far_ref, ka_ref, kb_ref, qa_ref, qb_ref, fa_ref, fb_ref, o_ref,
+                  turned, rows, sems):
     hd = HEAD_DIM
+    tiles = o_ref.shape[1] // TILE
+    sources = ((ka_ref, 0), (kb_ref, 0), (qa_ref, 0), (qb_ref, 0),
+               (fa_ref, 0), (fb_ref, 0), (fa_ref, hd), (fb_ref, hd))
+
+    def tile(i):
+        return pl.ds(pl.multiple_of(i * TILE, TILE), TILE)
+
+    def copies(i):
+        return [
+            pltpu.make_async_copy(
+                ref.at[tile(i), pl.ds(col, hd)], rows.at[tile(i), pl.ds(j * hd, hd)], sems.at[i, j]
+            )
+            for j, (ref, col) in enumerate(sources)
+        ]
+
+    @pl.loop(0, tiles)
+    def _(i):
+        for copy in copies(i):
+            copy.start()
+
     turned[: 4 * hd] = own_ref[...].T
     turned[4 * hd :] = far_ref[...].T
 
-    @pl.loop(0, o_ref.shape[1] // TILE)
+    @pl.loop(0, tiles)
     def _(i):
-        spot = pl.ds(pl.multiple_of(i * TILE, TILE), TILE)
-        rows = jnp.concatenate(
-            [ka_ref[spot, :], kb_ref[spot, :], qa_ref[spot, :], qb_ref[spot, :],
-             fa_ref[spot, :hd], fb_ref[spot, :hd], fa_ref[spot, hd:], fb_ref[spot, hd:]], 1)
-        acc = jnp.dot(rows, turned[...], preferred_element_type=f32)
-        o_ref[:, spot] = acc.astype(bf16).T
+        for copy in copies(i):
+            copy.wait()
+        acc = jnp.dot(rows[tile(i), :], turned[...], preferred_element_type=f32)
+        o_ref[:, tile(i)] = acc.astype(bf16).T
 
 
 def token_terms(own, far, narrow, wide):
@@ -165,11 +204,15 @@
     width = wide[0].shape[0]
     return pl.pallas_call(
         tokens_kernel,
-        in_specs=[near()] * 8,
+        in_specs=[near(), near()] + [far_off()] * 4 + [pl.BlockSpec(memory_space=pl.ANY)] * 2,
         out_specs=near(),
         out_shape=jax.ShapeDtypeStruct((rows, width), bf16),
-        scratch_shapes=[pltpu.VMEM((2 * cols, rows), bf16)],
-        compiler_params=limit(12),
+        scratch_shapes=[
+            pltpu.VMEM((2 * cols, rows), bf16),
+            pltpu.VMEM((width, 2 * cols), bf16),
+            pltpu.SemaphoreType.DMA((width // TILE, 8)),
+        ],
+        compiler_params=limit(52),
         name="token_terms",
     )(own, far, *narrow, *wide)
 

time: 228 us -> 223 us (0.978)
  local copies, waits for them, and re-layouts: 17.9 us -> 4.72 us
  Pallas kernels: 22.4 us -> 26.5 us
  waiting for transfers between devices: 85.5 us -> 89.2 us
    unnamed x51 -> x33, local copies, waits for them, and re-layouts: 13.8 us -> 1.67 us
    ppermute x31, waiting for transfers between devices: 71.6 us -> 79.7 us  [seq_move(): return lax.ppermute(block, 'seq', pairs)]
    all_to_all x1, waiting for transfers between devices: 4.39 us -> 0.01 us  [per_device(): lax.all_to_all(d_part.reshape(4, tok_rows // 8, -1), 'head', split_axis=0...]
    pallas_call x3, Pallas kernels: 12.3 us -> 16.5 us  [the longest x2 8.7 us: weight_terms(): pl.pallas_call(term_kernel, in_specs=[far_off(), near()], out_specs=[near...]
  transfers between devices with their start and end apart: 38 -> 38, of which waited for: 21 -> 20; matrix products, arithmetic and copies ran while one was open for 7% -> 7% of each run, Pallas kernels for 6% -> 8%
where the time goes in v1:
time: 223 us; the launch traced here: 220 us
  waiting for transfers between devices  89.2 us (40%)
  starting transfers between devices  80.2 us (36%)
  Pallas kernels  26.5 us (12%)
  other arithmetic  10.9 us (5%)
  matrix products  6.23 us (3%)
  local copies, waits for them, and re-layouts  4.72 us (2%)
    ppermute x31, waiting for transfers between devices, seq_move(): return lax.ppermute(block, 'seq', pairs)  79.7 us
    ppermute x31, starting transfers between devices, seq_move(): return lax.ppermute(block, 'seq', pairs)  53.4 us
    ppermute x4, starting transfers between devices, shifted(): return lax.ppermute(block, 'seq', route)  11.3 us
    ppermute x2, starting transfers between devices, head_move(): return lax.ppermute(block, 'head', pairs)  10.8 us
    pallas_call x2, Pallas kernels, weight_terms(): pl.pallas_call(term_kernel, in_specs=[far_off(), near()], out_specs=[near...  8.7 us
    pallas_call x1, Pallas kernels, attend(): pl.pallas_call(attend_kernel, grid_spec=pltpu.PrefetchScalarGridSpec(num_...  8.19 us
    pallas_call x1, Pallas kernels, token_terms(): pl.pallas_call(tokens_kernel, in_specs=[near(), near()] + [far_off()] * 4...  7.76 us
    ppermute x4, waiting for transfers between devices, shifted(): return lax.ppermute(block, 'seq', route)  4.92 us
  transfers between devices with their start and end apart: 38, of which 20 were waited for; matrix products, arithmetic and copies ran while one was open for 7% of the time, Pallas kernels for 8%

profile of v1, /device:TPU:1, one launch (start us, length us, event | category | flops | bytes accessed | tf_op | source)
XLA Modules:
  0.0 219.9 jit_solution(17730768935113748008)
XLA Ops:
  0.6 1.2 convert_element_type.106
  2.0 3.3 %collective-permute-start = (bf16[168,256]{1,0:T(8,128)(2,1)S(1)}, bf16[168,256]{1,0:T(8,128)(2,1)S(1)}, u32[]{:S(2)}, u32[]{:S(2)}) collective-permute-start(bf16[168,256]{1,0:T(8,128)(2,1)S(1)} %pad_maximum_fusion.5), channel_id=1, source_target_pairs={{0,8},{8,0},{16,24},{24,16},{32,40},{40,32},{48,56},{56,48},{64,72... | collective-permute-start | bytes 258056 | tf_op jit(solution)/shard_map/ppermute | solution.py:32
  5.3 0.9 collective-permute-done
  6.5 2.8 %collective-permute-start.2 = (bf16[336,256]{1,0:T(8,128)(2,1)S(1)}, bf16[336,256]{1,0:T(8,128)(2,1)S(1)}, u32[]{:S(2)}, u32[]{:S(2)}) collective-permute-start(bf16[336,256]{1,0:T(8,128)(2,1)S(1)} %pad_maximum_fusion.4), channel_id=1, source_target_pairs={{0,32},{8,40},{16,48},{24,56},{32,0},{40,8},{48,16},{56,24},{64,96... | collective-permute-start | bytes 516104 | tf_op jit(solution)/shard_map/ppermute | solution.py:32
  9.3 0.7 collective-permute-start.3
  10.0 3.8 %collective-permute-done.1 = bf16[336,256]{1,0:T(8,128)(2,1)S(1)} collective-permute-done((bf16[336,256]{1,0:T(8,128)(2,1)S(1)}, bf16[336,256]{1,0:T(8,128)(2,1)S(1)}, u32[]{:S(2)}, u32[]{:S(2)}) %collective-permute-start.1) | collective-permute-done | bytes 172064 | tf_op jit(solution)/shard_map/ppermute | solution.py:32
  13.8 7.3 %collective-permute-done.2 = bf16[336,256]{1,0:T(8,128)(2,1)S(1)} collective-permute-done((bf16[336,256]{1,0:T(8,128)(2,1)S(1)}, bf16[336,256]{1,0:T(8,128)(2,1)S(1)}, u32[]{:S(2)}, u32[]{:S(2)}) %collective-permute-start.2) | collective-permute-done | bytes 172064 | tf_op jit(solution)/shard_map/ppermute | solution.py:32
  21.3 1.3 collective-permute-start.4
  22.6 1.4 collective-permute-start.5
  24.1 1.6 collective-permute-start.6
  25.6 5.3 %collective-permute-done.4 = bf16[1344,128]{1,0:T(8,128)(2,1)S(1)} collective-permute-done((bf16[1344,128]{1,0:T(8,128)(2,1)S(1)}, bf16[1344,128]{1,0:T(8,128)(2,1)S(1)}, u32[]{:S(2)}, u32[]{:S(2)}) %collective-permute-start.4) | collective-permute-done | bytes 344096 | tf_op jit(solution)/shard_map/ppermute | solution.py:32
  31.5 8.6 %collective-permute-done.6 = bf16[1344,128]{1,0:T(8,128)(2,1)S(1)} collective-permute-done((bf16[1344,128]{1,0:T(8,128)(2,1)S(1)}, bf16[1344,128]{1,0:T(8,128)(2,1)S(1)}, u32[]{:S(2)}, u32[]{:S(2)}) %collective-permute-start.6) | collective-permute-done | bytes 344096 | tf_op jit(solution)/shard_map/ppermute | solution.py:32
  40.1 1.5 collective-permute-start.7
  41.6 0.9 collective-permute-start.8
  42.5 1.8 collective-permute-start.9
  44.5 4.6 %fusion.11 = f32[512,256]{1,0:T(8,128)S(1)} fusion(bf16[512,5376]{1,0:T(8,128)(2,1)} %n_ref.3, bf16[5376,128]{1,0:T(8,128)(2,1)S(1)} %collective-permute-done.7.kb_ref, bf16[5376,128]{1,0:T(8,128)(2,1)S(1)} %bitcast.84), kind=kOutput, calls=%fused_computation.12 | convolution fusion | flops 1414791168 | bytes 8781824 | tf_op jit(solution)/shard_map/dot_general | solution.py:360
  49.6 2.8 %collective-permute-done.8 = bf16[1344,128]{1,0:T(8,128)(2,1)S(1)} collective-permute-done((bf16[1344,128]{1,0:T(8,128)(2,1)S(1)}, bf16[1344,128]{1,0:T(8,128)(2,1)S(1)}, u32[]{:S(2)}, u32[]{:S(2)}) %collective-permute-start.8) | collective-permute-done | bytes 344096 | tf_op jit(solution)/shard_map/ppermute | solution.py:32
  52.3 7.6 %collective-permute-done.10 = bf16[1344,128]{1,0:T(8,128)(2,1)S(1)} collective-permute-done((bf16[1344,128]{1,0:T(8,128)(2,1)S(1)}, bf16[1344,128]{1,0:T(8,128)(2,1)S(1)}, u32[]{:S(2)}, u32[]{:S(2)}) %collective-permute-start.10) | collective-permute-done | bytes 344096 | tf_op jit(solution)/shard_map/ppermute | solution.py:32
  60.3 1.0 collective-permute-start.11
  61.4 5.6 %collective-permute-start.12 = (bf16[336,256]{1,0:T(8,128)(2,1)S(1)}, bf16[336,256]{1,0:T(8,128)(2,1)S(1)}, u32[]{:S(2)}, u32[]{:S(2)}) collective-permute-start(bf16[336,256]{1,0:T(8,128)(2,1)S(1)} %pad_maximum_fusion.4), channel_id=1, source_target_pairs={{0,4},{1,5},{2,6},{3,7},{4,0},{5,1},{6,2},{7,3},{8,12},{9,13},{10,... | collective-permute-start | bytes 516104 | tf_op jit(solution)/shard_map/ppermute | solution.py:40
  66.9 4.6 %collective-permute-done.12 = bf16[336,256]{1,0:T(8,128)(2,1)S(1)} collective-permute-done((bf16[336,256]{1,0:T(8,128)(2,1)S(1)}, bf16[336,256]{1,0:T(8,128)(2,1)S(1)}, u32[]{:S(2)}, u32[]{:S(2)}) %collective-permute-start.12) | collective-permute-done | bytes 172064 | tf_op jit(solution)/shard_map/ppermute | solution.py:40
  71.5 7.8 %collective-permute-start.13 = (bf16[336,256]{1,0:T(8,128)(2,1)S(1)}, bf16[336,256]{1,0:T(8,128)(2,1)S(1)}, u32[]{:S(2)}, u32[]{:S(2)}) collective-permute-start(bf16[336,256]{1,0:T(8,128)(2,1)S(1)} %collective-permute-done.12), channel_id=1, source_target_pairs={{0,16},{8,24},{16,32},{24,40},{32,48},{40,56},{48,0},{56,8},{64,80... | collective-permute-start | bytes 516104 | tf_op jit(solution)/shard_map/ppermute | solution.py:32
  80.2 2.1 collective-permute-start.15
  82.6 8.3 %collective-permute-done.14 = bf16[336,256]{1,0:T(8,128)(2,1)S(1)} collective-permute-done((bf16[336,256]{1,0:T(8,128)(2,1)S(1)}, bf16[336,256]{1,0:T(8,128)(2,1)S(1)}, u32[]{:S(2)}, u32[]{:S(2)}) %collective-permute-start.14) | collective-permute-done | bytes 172064 | tf_op jit(solution)/shard_map/ppermute | solution.py:32
  90.9 5.9 %collective-permute-start.16 = (bf16[512,256]{1,0:T(8,128)(2,1)S(1)}, bf16[512,256]{1,0:T(8,128)(2,1)S(1)}, u32[]{:S(2)}, u32[]{:S(2)}) collective-permute-start(bf16[512,256]{1,0:T(8,128)(2,1)S(1)} %pad_maximum_fusion.2.own_ref), channel_id=1, source_target_pairs={{0,16},{8,24},{16,32},{24,40},{32,48},{40,56},{48,64},{56,72},{64,... | collective-permute-start | bytes 786440 | tf_op jit(solution)/shard_map/ppermute | solution.py:49
  96.8 2.3 %collective-permute-start.17 = (bf16[512,256]{1,0:T(8,128)(2,1)S(1)}, bf16[512,256]{1,0:T(8,128)(2,1)S(1)}, u32[]{:S(2)}, u32[]{:S(2)}) collective-permute-start(bf16[512,256]{1,0:T(8,128)(2,1)S(1)} %pad_maximum_fusion.2.own_ref), channel_id=1, source_target_pairs={{0,8},{8,16},{16,24},{24,32},{32,40},{40,48},{48,56},{56,64},{64,7... | collective-permute-start | bytes 786440 | tf_op jit(solution)/shard_map/ppermute | solution.py:49
  99.1 1.6 fusion.8.q_ref
  100.7 1.2 collective-permute-done.16.two_ref
  101.9 3.8 %collective-permute-done.17.one_ref = bf16[512,256]{1,0:T(8,128)(2,1)S(1)} collective-permute-done((bf16[512,256]{1,0:T(8,128)(2,1)S(1)}, bf16[512,256]{1,0:T(8,128)(2,1)S(1)}, u32[]{:S(2)}, u32[]{:S(2)}) %collective-permute-start.17) | collective-permute-done | bytes 262176 | tf_op jit(solution)/shard_map/ppermute | solution.py:49
  105.7 8.2 %attend.1 = (bf16[512,256]{1,0:T(8,128)(2,1)}, bf16[512,256]{1,0:T(8,128)(2,1)S(1)}, bf16[512,256]{1,0:T(8,128)(2,1)S(1)}, bf16[512,256]{1,0:T(8,128)(2,1)S(1)}, f32[512,256]{1,0:T(8,128)S(1)}) custom-call(s32[2]{0:T(128)S(1)} %pad_add_fusion.pos_ref, f32[1]{0:T(128)S(6)} %convert_element_type.105.power_ref, f32[512,256]{1,0:T(8,128)S(1)} %fusion.8.q_ref, ...), custom_call_target="tpu_custom_call" | custom-call | tf_op jit(solution)/shard_map/attend/pallas_call | solution.py:278
  113.9 1.3 collective-permute-start.19
  115.1 1.9 collective-permute-start.18
  117.1 6.6 %collective-permute-start.21 = (bf16[1344,256]{1,0:T(8,128)(2,1)}, bf16[1344,256]{1,0:T(8,128)(2,1)S(1)}, u32[]{:S(2)}, u32[]{:S(2)}) collective-permute-start(bf16[1344,256]{1,0:T(8,128)(2,1)} %bitcast.101), channel_id=1, source_target_pairs={{0,64},{8,72},{16,80},{24,88},{32,96},{40,104},{48,112},{56,120},{... | collective-permute-start | bytes 2064392 | tf_op jit(solution)/shard_map/ppermute | solution.py:32
  123.8 2.6 %collective-permute-start.23 = (bf16[1344,256]{1,0:T(8,128)(2,1)}, bf16[1344,256]{1,0:T(8,128)(2,1)S(1)}, u32[]{:S(2)}, u32[]{:S(2)}) collective-permute-start(bf16[1344,256]{1,0:T(8,128)(2,1)} %bitcast.103), channel_id=1, source_target_pairs={{0,128},{8,136},{16,144},{24,152},{32,160},{40,168},{48,176},{56,1... | collective-permute-start | bytes 2064392 | tf_op jit(solution)/shard_map/ppermute | solution.py:32
  126.4 4.3 %weight_terms.2 = (bf16[5376,128]{1,0:T(8,128)(2,1)S(1)}, bf16[5376,128]{1,0:T(8,128)(2,1)S(1)}) custom-call(bf16[512,5376]{1,0:T(8,128)(2,1)} %n_ref.3, bf16[512,256]{1,0:T(8,128)(2,1)S(1)} %get-tuple-element.48.g_ref), custom_call_target="tpu_custom_call" | custom-call | tf_op jit(solution)/shard_map/weight_terms/pallas_call | solution.py:153
  130.7 0.9 collective-permute-start.25
  132.3 5.2 %collective-permute-start.20 = (bf16[256,512]{1,0:T(8,128)(2,1)S(1)}, bf16[256,512]{1,0:T(8,128)(2,1)S(1)}, u32[]{:S(2)}, u32[]{:S(2)}) collective-permute-start(bf16[256,512]{1,0:T(8,128)(2,1)S(1)} %get-tuple-element.89), channel_id=1, source_target_pairs={{0,4},{1,5},{2,6},{3,7},{4,0},{5,1},{6,2},{7,3},{8,12},{9,13},{10,... | collective-permute-start | bytes 786440 | tf_op jit(solution)/shard_map/ppermute | solution.py:40
  137.6 4.4 %weight_terms.3 = (bf16[5376,128]{1,0:T(8,128)(2,1)S(1)}, bf16[5376,128]{1,0:T(8,128)(2,1)S(1)}) custom-call(bf16[512,5376]{1,0:T(8,128)(2,1)} %n_ref.3, bf16[512,256]{1,0:T(8,128)(2,1)S(1)} %pad_maximum_fusion.3.g_ref), custom_call_target="tpu_custom_call" | custom-call | tf_op jit(solution)/shard_map/weight_terms/pallas_call | solution.py:153
  142.0 13.7 %collective-permute-done.23 = bf16[1344,256]{1,0:T(8,128)(2,1)S(1)} collective-permute-done((bf16[1344,256]{1,0:T(8,128)(2,1)}, bf16[1344,256]{1,0:T(8,128)(2,1)S(1)}, u32[]{:S(2)}, u32[]{:S(2)}) %collective-permute-start.23) | collective-permute-done | bytes 688160 | tf_op jit(solution)/shard_map/ppermute | solution.py:32
  156.1 0.7 collective-permute-start.24
  156.9 1.8 add_convert_fusion.1
  158.8 1.1 collective-permute-start.26
  159.9 1.8 collective-permute-start.27
  161.7 1.7 collective-permute-done.29
  163.4 1.8 collective-permute-start.28
  165.2 0.4 add_convert_fusion
  165.6 1.0 dynamic-slice_bitcast_fusion
  166.6 1.5 collective-permute-start.30
  168.1 1.1 collective-permute-done.26
  169.1 1.3 collective-permute-start.31
  170.4 1.6 copy-done.6
  172.2 7.8 %token_terms.1 = bf16[256,5376]{1,0:T(8,128)(2,1)} custom-call(bf16[256,512]{1,0:T(8,128)(2,1)S(1)} %get-tuple-element.90.own_ref, bf16[256,512]{1,0:T(8,128)(2,1)S(1)} %collective-permute-done.20.far_ref, bf16[5376,128]{1,0:T(8,128)(2,1)S(1)} %bitcast.85, bf16[5376,128]{1,0:T(8,128)(2,1)} %copy-done.9, bf16[5376,128]{1,0:T(8,128)(2,1)} %bitcast.96, ...), custom_call_target="tpu_custom_call" | custom-call | tf_op jit(solution)/shard_map/token_terms/pallas_call | solution.py:205
  180.0 4.7 %all-to-all-start = ((bf16[4,64,5376]{2,1,0:T(8,128)(2,1)}), bf16[4,64,5376]{2,1,0:T(8,128)(2,1)}, u32[]{:S(2)}, u32[]{:S(2)}) async-start(bf16[4,64,5376]{2,1,0:T(8,128)(2,1)} %bitcast.91), calls=%async_computation | async-start | bytes 5505024 | tf_op jit(solution)/shard_map/all_to_all | solution.py:409
  185.0 7.3 %collective-permute-done.32 = bf16[1344,128]{1,0:T(8,128)(2,1)} collective-permute-done((bf16[1344,128]{1,0:T(8,128)(2,1)}, bf16[1344,128]{1,0:T(8,128)(2,1)}, u32[]{:S(2)}, u32[]{:S(2)}) %collective-permute-start.32) | collective-permute-done | bytes 344096 | tf_op jit(solution)/shard_map/ppermute | solution.py:32
  192.3 1.3 add_convert_fusion.3
  193.6 1.4 add_convert_fusion.4
  195.2 5.7 %collective-permute-start.34 = (bf16[336,256]{1,0:T(8,128)(2,1)S(1)}, bf16[336,256]{1,0:T(8,128)(2,1)S(1)}, u32[]{:S(2)}, u32[]{:S(2)}) collective-permute-start(bf16[336,256]{1,0:T(8,128)(2,1)S(1)} %get-tuple-element.86), channel_id=1, source_target_pairs={{0,48},{8,56},{16,0},{24,8},{32,16},{40,24},{48,32},{56,40},{64,11... | collective-permute-start | bytes 516104 | tf_op jit(solution)/shard_map/ppermute | solution.py:32
  201.1 3.2 %collective-permute-done.34 = bf16[336,256]{1,0:T(8,128)(2,1)S(1)} collective-permute-done((bf16[336,256]{1,0:T(8,128)(2,1)S(1)}, bf16[336,256]{1,0:T(8,128)(2,1)S(1)}, u32[]{:S(2)}, u32[]{:S(2)}) %collective-permute-start.34) | collective-permute-done | bytes 172064 | tf_op jit(solution)/shard_map/ppermute | solution.py:32
  204.3 7.5 %collective-permute-done.33 = bf16[336,256]{1,0:T(8,128)(2,1)S(1)} collective-permute-done((bf16[336,256]{1,0:T(8,128)(2,1)S(1)}, bf16[336,256]{1,0:T(8,128)(2,1)S(1)}, u32[]{:S(2)}, u32[]{:S(2)}) %collective-permute-start.33) | collective-permute-done | bytes 172064 | tf_op jit(solution)/shard_map/ppermute | solution.py:32
  211.9 1.9 collective-permute-start.36
  213.8 0.6 dynamic_slice.56
  214.4 0.7 pad_add_fusion.1.info_ref
  215.2 1.9 adam_step.1
  217.0 2.9 %fusion.14 = bf16[64,5376]{1,0:T(8,128)(2,1)} fusion(bf16[4,64,5376]{2,1,0:T(8,128)(2,1)} %all-to-all-done), kind=kLoop, calls=%fused_computation.13 | loop fusion | flops 2752512 | bytes 3440640 | tf_op jit(solution)/shard_map/add | solution.py:83
  (107 shorter events, 4.7 us)
Async XLA Ops:
  2.0 4.2 %collective-permute-start = (bf16[168,256]{1,0:T(8,128)(2,1)S(1)}, bf16[168,256]{1,0:T(8,128)(2,1)S(1)}, u32[]{:S(2)}, u32[]{:S(2)}) collective-permute-start(bf16[168,256]{1,0:T(8,128)(2,1)S(1)} %pad_maximum_fusion.5), channel_id=1, source_target_pairs={{0,8},{8,0},{16,24},{24,16},{32,40},{40,32},{48,56},{56,48},{64,72... | collective-permute-start | bytes 258056 | tf_op jit(solution)/shard_map/ppermute | solution.py:32
  6.3 7.5 %collective-permute-start.1 = (bf16[336,256]{1,0:T(8,128)(2,1)S(1)}, bf16[336,256]{1,0:T(8,128)(2,1)S(1)}, u32[]{:S(2)}, u32[]{:S(2)}) collective-permute-start(bf16[336,256]{1,0:T(8,128)(2,1)S(1)} %pad_maximum_fusion.4), channel_id=1, source_target_pairs={{0,16},{8,24},{16,32},{24,40},{32,48},{40,56},{48,0},{56,8},{64,80... | collective-permute-start | bytes 516104 | tf_op jit(solution)/shard_map/ppermute | solution.py:32
  6.5 14.7 %collective-permute-start.2 = (bf16[336,256]{1,0:T(8,128)(2,1)S(1)}, bf16[336,256]{1,0:T(8,128)(2,1)S(1)}, u32[]{:S(2)}, u32[]{:S(2)}) collective-permute-start(bf16[336,256]{1,0:T(8,128)(2,1)S(1)} %pad_maximum_fusion.4), channel_id=1, source_target_pairs={{0,32},{8,40},{16,48},{24,56},{32,0},{40,8},{48,16},{56,24},{64,96... | collective-permute-start | bytes 516104 | tf_op jit(solution)/shard_map/ppermute | solution.py:32
  9.3 11.9 %collective-permute-start.3 = (bf16[336,256]{1,0:T(8,128)(2,1)S(1)}, bf16[336,256]{1,0:T(8,128)(2,1)S(1)}, u32[]{:S(2)}, u32[]{:S(2)}) collective-permute-start(bf16[336,256]{1,0:T(8,128)(2,1)S(1)} %pad_maximum_fusion.4), channel_id=1, source_target_pairs={{0,48},{8,56},{16,0},{24,8},{32,16},{40,24},{48,32},{56,40},{64,11... | collective-permute-start | bytes 516104 | tf_op jit(solution)/shard_map/ppermute | solution.py:32
  21.3 9.6 %collective-permute-start.4 = (bf16[1344,128]{1,0:T(8,128)(2,1)S(1)}, bf16[1344,128]{1,0:T(8,128)(2,1)S(1)}, u32[]{:S(2)}, u32[]{:S(2)}) collective-permute-start(bf16[1344,128]{1,0:T(8,128)(2,1)S(1)} %get-tuple-element.87), channel_id=1, source_target_pairs={{0,64},{8,72},{16,80},{24,88},{32,96},{40,104},{48,112},{56,120},{... | collective-permute-start | bytes 1032200 | tf_op jit(solution)/shard_map/ppermute | solution.py:32
  22.6 8.8 %collective-permute-start.5 = (bf16[1344,128]{1,0:T(8,128)(2,1)S(1)}, bf16[1344,128]{1,0:T(8,128)(2,1)S(1)}, u32[]{:S(2)}, u32[]{:S(2)}) collective-permute-start(bf16[1344,128]{1,0:T(8,128)(2,1)S(1)} %get-tuple-element.87), channel_id=1, source_target_pairs={{0,192},{8,200},{16,208},{24,216},{32,224},{40,232},{48,240},{56,2... | collective-permute-start | bytes 1032200 | tf_op jit(solution)/shard_map/ppermute | solution.py:32
  24.1 16.0 %collective-permute-start.6 = (bf16[1344,128]{1,0:T(8,128)(2,1)S(1)}, bf16[1344,128]{1,0:T(8,128)(2,1)S(1)}, u32[]{:S(2)}, u32[]{:S(2)}) collective-permute-start(bf16[1344,128]{1,0:T(8,128)(2,1)S(1)} %get-tuple-element.87), channel_id=1, source_target_pairs={{0,128},{8,136},{16,144},{24,152},{32,160},{40,168},{48,176},{56,1... | collective-permute-start | bytes 1032200 | tf_op jit(solution)/shard_map/ppermute | solution.py:32
  40.1 59.0 %slice-start = ((s8[5505024]{0:T(1024)(128)(4,1)}), s8[4194304]{0:T(1024)(128)(4,1)S(1)}, s32[]{:S(2)}) async-start(s8[5505024]{0:T(1024)(128)(4,1)} %bitcast.89), calls=%async_computation.1 | async-start | bytes 8388608
  40.1 4.4 %collective-permute-start.7 = (bf16[5376,128]{1,0:T(8,128)(2,1)S(1)}, bf16[5376,128]{1,0:T(8,128)(2,1)S(1)}, u32[]{:S(2)}, u32[]{:S(2)}) collective-permute-start(bf16[5376,128]{1,0:T(8,128)(2,1)S(1)} %bitcast.83), channel_id=1, source_target_pairs={{0,8},{8,0},{16,24},{24,16},{32,40},{40,32},{48,56},{56,48},{64,72... | collective-permute-start | bytes 4128776 | tf_op jit(solution)/shard_map/ppermute | solution.py:32
  41.6 57.5 %slice-start.1 = ((s8[5505024]{0:T(1024)(128)(4,1)}), s8[1310720]{0:T(1024)(128)(4,1)S(1)}, s32[]{:S(2)}) async-start(s8[5505024]{0:T(1024)(128)(4,1)} %bitcast.89), calls=%async_computation.2 | async-start | bytes 2621440
  41.6 10.7 %collective-permute-start.8 = (bf16[1344,128]{1,0:T(8,128)(2,1)S(1)}, bf16[1344,128]{1,0:T(8,128)(2,1)S(1)}, u32[]{:S(2)}, u32[]{:S(2)}) collective-permute-start(bf16[1344,128]{1,0:T(8,128)(2,1)S(1)} %get-tuple-element.36), channel_id=1, source_target_pairs={{0,64},{8,72},{16,80},{24,88},{32,96},{40,104},{48,112},{56,120},{... | collective-permute-start | bytes 1032200 | tf_op jit(solution)/shard_map/ppermute | solution.py:32
  42.5 9.9 %collective-permute-start.9 = (bf16[1344,128]{1,0:T(8,128)(2,1)S(1)}, bf16[1344,128]{1,0:T(8,128)(2,1)S(1)}, u32[]{:S(2)}, u32[]{:S(2)}) collective-permute-start(bf16[1344,128]{1,0:T(8,128)(2,1)S(1)} %get-tuple-element.36), channel_id=1, source_target_pairs={{0,192},{8,200},{16,208},{24,216},{32,224},{40,232},{48,240},{56,2... | collective-permute-start | bytes 1032200 | tf_op jit(solution)/shard_map/ppermute | solution.py:32
  44.3 15.7 %collective-permute-start.10 = (bf16[1344,128]{1,0:T(8,128)(2,1)S(1)}, bf16[1344,128]{1,0:T(8,128)(2,1)S(1)}, u32[]{:S(2)}, u32[]{:S(2)}) collective-permute-start(bf16[1344,128]{1,0:T(8,128)(2,1)S(1)} %get-tuple-element.36), channel_id=1, source_target_pairs={{0,128},{8,136},{16,144},{24,152},{32,160},{40,168},{48,176},{56,1... | collective-permute-start | bytes 1032200 | tf_op jit(solution)/shard_map/ppermute | solution.py:32
  44.5 4.7 %copy-start.9 = (bf16[5376,128]{1,0:T(8,128)(2,1)}, bf16[5376,128]{1,0:T(8,128)(2,1)S(1)}, u32[]{:S(2)}) copy-start(bf16[5376,128]{1,0:T(8,128)(2,1)S(1)} %collective-permute-done.7.kb_ref) | copy-start | bytes 4128772
  60.3 40.4 %copy-start.5 = (bf16[4,1344,128]{2,1,0:T(8,128)(2,1)}, bf16[4,1344,128]{2,1,0:T(8,128)(2,1)S(1)}, u32[]{:S(2)}) copy-start(bf16[4,1344,128]{2,1,0:T(8,128)(2,1)S(1)} %bitcast_dynamic-update-slice_fusion.3) | copy-start | bytes 4128772
  60.3 38.8 %collective-permute-start.11 = (bf16[5376,128]{1,0:T(8,128)(2,1)S(1)}, bf16[5376,128]{1,0:T(8,128)(2,1)S(1)}, u32[]{:S(2)}, u32[]{:S(2)}) collective-permute-start(bf16[5376,128]{1,0:T(8,128)(2,1)S(1)} %bitcast.94), channel_id=1, source_target_pairs={{0,8},{8,0},{16,24},{24,16},{32,40},{40,32},{48,56},{56,48},{64,72... | collective-permute-start | bytes 4128776 | tf_op jit(solution)/shard_map/ppermute | solution.py:32
  61.4 10.1 %collective-permute-start.12 = (bf16[336,256]{1,0:T(8,128)(2,1)S(1)}, bf16[336,256]{1,0:T(8,128)(2,1)S(1)}, u32[]{:S(2)}, u32[]{:S(2)}) collective-permute-start(bf16[336,256]{1,0:T(8,128)(2,1)S(1)} %pad_maximum_fusion.4), channel_id=1, source_target_pairs={{0,4},{1,5},{2,6},{3,7},{4,0},{5,1},{6,2},{7,3},{8,12},{9,13},{10,... | collective-permute-start | bytes 516104 | tf_op jit(solution)/shard_map/ppermute | solution.py:40
  71.5 11.0 %collective-permute-start.13 = (bf16[336,256]{1,0:T(8,128)(2,1)S(1)}, bf16[336,256]{1,0:T(8,128)(2,1)S(1)}, u32[]{:S(2)}, u32[]{:S(2)}) collective-permute-start(bf16[336,256]{1,0:T(8,128)(2,1)S(1)} %collective-permute-done.12), channel_id=1, source_target_pairs={{0,16},{8,24},{16,32},{24,40},{32,48},{40,56},{48,0},{56,8},{64,80... | collective-permute-start | bytes 516104 | tf_op jit(solution)/shard_map/ppermute | solution.py:32
  80.0 10.8 %collective-permute-start.14 = (bf16[336,256]{1,0:T(8,128)(2,1)S(1)}, bf16[336,256]{1,0:T(8,128)(2,1)S(1)}, u32[]{:S(2)}, u32[]{:S(2)}) collective-permute-start(bf16[336,256]{1,0:T(8,128)(2,1)S(1)} %collective-permute-done.12), channel_id=1, source_target_pairs={{0,32},{8,40},{16,48},{24,56},{32,0},{40,8},{48,16},{56,24},{64,96... | collective-permute-start | bytes 516104 | tf_op jit(solution)/shard_map/ppermute | solution.py:32
  80.2 10.6 %collective-permute-start.15 = (bf16[336,256]{1,0:T(8,128)(2,1)S(1)}, bf16[336,256]{1,0:T(8,128)(2,1)S(1)}, u32[]{:S(2)}, u32[]{:S(2)}) collective-permute-start(bf16[336,256]{1,0:T(8,128)(2,1)S(1)} %collective-permute-done.12), channel_id=1, source_target_pairs={{0,48},{8,56},{16,0},{24,8},{32,16},{40,24},{48,32},{56,40},{64,11... | collective-permute-start | bytes 516104 | tf_op jit(solution)/shard_map/ppermute | solution.py:32
  90.9 8.2 %copy-start.7 = (bf16[4,336,256]{2,1,0:T(8,128)(2,1)}, bf16[4,336,256]{2,1,0:T(8,128)(2,1)S(1)}, u32[]{:S(2)}) copy-start(bf16[4,336,256]{2,1,0:T(8,128)(2,1)S(1)} %bitcast_dynamic-update-slice_fusion.9) | copy-start | bytes 2064388
  90.9 11.0 %collective-permute-start.16 = (bf16[512,256]{1,0:T(8,128)(2,1)S(1)}, bf16[512,256]{1,0:T(8,128)(2,1)S(1)}, u32[]{:S(2)}, u32[]{:S(2)}) collective-permute-start(bf16[512,256]{1,0:T(8,128)(2,1)S(1)} %pad_maximum_fusion.2.own_ref), channel_id=1, source_target_pairs={{0,16},{8,24},{16,32},{24,40},{32,48},{40,56},{48,64},{56,72},{64,... | collective-permute-start | bytes 786440 | tf_op jit(solution)/shard_map/ppermute | solution.py:49
  96.8 8.9 %collective-permute-start.17 = (bf16[512,256]{1,0:T(8,128)(2,1)S(1)}, bf16[512,256]{1,0:T(8,128)(2,1)S(1)}, u32[]{:S(2)}, u32[]{:S(2)}) collective-permute-start(bf16[512,256]{1,0:T(8,128)(2,1)S(1)} %pad_maximum_fusion.2.own_ref), channel_id=1, source_target_pairs={{0,8},{8,16},{16,24},{24,32},{32,40},{40,48},{48,56},{56,64},{64,7... | collective-permute-start | bytes 786440 | tf_op jit(solution)/shard_map/ppermute | solution.py:49
  99.1 6.6 %copy-start.3 = (bf16[512,256]{1,0:T(8,128)(2,1)S(1)}, bf16[512,256]{1,0:T(8,128)(2,1)}, u32[]{:S(2)}) copy-start(bf16[512,256]{1,0:T(8,128)(2,1)} %cot_ref.1) | copy-start | bytes 786436
  99.1 1.6 copy-start.10
  113.9 16.9 %collective-permute-start.19 = (bf16[512,256]{1,0:T(8,128)(2,1)S(1)}, bf16[512,256]{1,0:T(8,128)(2,1)S(1)}, u32[]{:S(2)}, u32[]{:S(2)}) collective-permute-start(bf16[512,256]{1,0:T(8,128)(2,1)S(1)} %get-tuple-element.47), channel_id=1, source_target_pairs={{16,0},{24,8},{32,16},{40,24},{48,32},{56,40},{64,48},{72,56},{80,... | collective-permute-start | bytes 786440 | tf_op jit(solution)/shard_map/ppermute | solution.py:49
  115.1 16.5 %collective-permute-start.18 = (bf16[512,256]{1,0:T(8,128)(2,1)S(1)}, bf16[512,256]{1,0:T(8,128)(2,1)S(1)}, u32[]{:S(2)}, u32[]{:S(2)}) collective-permute-start(bf16[512,256]{1,0:T(8,128)(2,1)S(1)} %get-tuple-element.46), channel_id=1, source_target_pairs={{8,0},{16,8},{24,16},{32,24},{40,32},{48,40},{56,48},{64,56},{72,6... | collective-permute-start | bytes 786440 | tf_op jit(solution)/shard_map/ppermute | solution.py:49
  117.1 24.8 %collective-permute-start.21 = (bf16[1344,256]{1,0:T(8,128)(2,1)}, bf16[1344,256]{1,0:T(8,128)(2,1)S(1)}, u32[]{:S(2)}, u32[]{:S(2)}) collective-permute-start(bf16[1344,256]{1,0:T(8,128)(2,1)} %bitcast.101), channel_id=1, source_target_pairs={{0,64},{8,72},{16,80},{24,88},{32,96},{40,104},{48,112},{56,120},{... | collective-permute-start | bytes 2064392 | tf_op jit(solution)/shard_map/ppermute | solution.py:32
  123.8 18.2 %collective-permute-start.22 = (bf16[1344,256]{1,0:T(8,128)(2,1)}, bf16[1344,256]{1,0:T(8,128)(2,1)S(1)}, u32[]{:S(2)}, u32[]{:S(2)}) collective-permute-start(bf16[1344,256]{1,0:T(8,128)(2,1)} %bitcast.102), channel_id=1, source_target_pairs={{0,192},{8,200},{16,208},{24,216},{32,224},{40,232},{48,240},{56,2... | collective-permute-start | bytes 2064392 | tf_op jit(solution)/shard_map/ppermute | solution.py:32
  123.8 31.9 %collective-permute-start.23 = (bf16[1344,256]{1,0:T(8,128)(2,1)}, bf16[1344,256]{1,0:T(8,128)(2,1)S(1)}, u32[]{:S(2)}, u32[]{:S(2)}) collective-permute-start(bf16[1344,256]{1,0:T(8,128)(2,1)} %bitcast.103), channel_id=1, source_target_pairs={{0,128},{8,136},{16,144},{24,152},{32,160},{40,168},{48,176},{56,1... | collective-permute-start | bytes 2064392 | tf_op jit(solution)/shard_map/ppermute | solution.py:32
  130.7 26.1 %collective-permute-start.25 = (bf16[5376,128]{1,0:T(8,128)(2,1)S(1)}, bf16[5376,128]{1,0:T(8,128)(2,1)}, u32[]{:S(2)}, u32[]{:S(2)}) collective-permute-start(bf16[5376,128]{1,0:T(8,128)(2,1)S(1)} %get-tuple-element.53), channel_id=1, source_target_pairs={{0,8},{8,0},{16,24},{24,16},{32,40},{40,32},{48,56},{56,48},{64,72... | collective-permute-start | bytes 4128776 | tf_op jit(solution)/shard_map/ppermute | solution.py:32
  132.3 34.3 %collective-permute-start.20 = (bf16[256,512]{1,0:T(8,128)(2,1)S(1)}, bf16[256,512]{1,0:T(8,128)(2,1)S(1)}, u32[]{:S(2)}, u32[]{:S(2)}) collective-permute-start(bf16[256,512]{1,0:T(8,128)(2,1)S(1)} %get-tuple-element.89), channel_id=1, source_target_pairs={{0,4},{1,5},{2,6},{3,7},{4,0},{5,1},{6,2},{7,3},{8,12},{9,13},{10,... | collective-permute-start | bytes 786440 | tf_op jit(solution)/shard_map/ppermute | solution.py:40
  137.5 18.2 %copy-start.8 = (bf16[4,336,256]{2,1,0:T(8,128)(2,1)S(1)}, bf16[4,336,256]{2,1,0:T(8,128)(2,1)}, u32[]{:S(2)}) copy-start(bf16[4,336,256]{2,1,0:T(8,128)(2,1)} %copy-done.7) | copy-start | bytes 2064388
  156.1 2.6 %copy-start.4 = (bf16[4,1344,256]{2,1,0:T(8,128)(2,1)}, bf16[4,1344,256]{2,1,0:T(8,128)(2,1)S(1)}, u32[]{:S(2)}) copy-start(bf16[4,1344,256]{2,1,0:T(8,128)(2,1)S(1)} %bitcast_dynamic-update-slice_fusion) | copy-start | bytes 8257540
  156.1 14.3 %collective-permute-start.24 = (bf16[5376,256]{1,0:T(8,128)(2,1)S(1)}, bf16[5376,256]{1,0:T(8,128)(2,1)S(1)}, u32[]{:S(2)}, u32[]{:S(2)}) collective-permute-start(bf16[5376,256]{1,0:T(8,128)(2,1)S(1)} %bitcast.92), channel_id=1, source_target_pairs={{0,8},{8,0},{16,24},{24,16},{32,40},{40,32},{48,56},{56,48},{64,72... | collective-permute-start | bytes 8257544 | tf_op jit(solution)/shard_map/ppermute | solution.py:32
  156.8 6.7 %collective-permute-start.29 = (bf16[5376,128]{1,0:T(8,128)(2,1)S(1)}, bf16[5376,128]{1,0:T(8,128)(2,1)S(1)}, u32[]{:S(2)}, u32[]{:S(2)}) collective-permute-start(bf16[5376,128]{1,0:T(8,128)(2,1)S(1)} %get-tuple-element.55), channel_id=1, source_target_pairs={{0,8},{8,0},{16,24},{24,16},{32,40},{40,32},{48,56},{56,48},{64,72... | collective-permute-start | bytes 4128776 | tf_op jit(solution)/shard_map/ppermute | solution.py:32
  158.8 10.3 %collective-permute-start.26 = (bf16[1344,128]{1,0:T(8,128)(2,1)S(1)}, bf16[1344,128]{1,0:T(8,128)(2,1)S(1)}, u32[]{:S(2)}, u32[]{:S(2)}) collective-permute-start(bf16[1344,128]{1,0:T(8,128)(2,1)S(1)} %get-tuple-element.82), channel_id=1, source_target_pairs={{0,64},{8,72},{16,80},{24,88},{32,96},{40,104},{48,112},{56,120},{... | collective-permute-start | bytes 1032200 | tf_op jit(solution)/shard_map/ppermute | solution.py:32
  159.9 24.8 %collective-permute-start.27 = (bf16[1344,128]{1,0:T(8,128)(2,1)S(1)}, bf16[1344,128]{1,0:T(8,128)(2,1)}, u32[]{:S(2)}, u32[]{:S(2)}) collective-permute-start(bf16[1344,128]{1,0:T(8,128)(2,1)S(1)} %get-tuple-element.81), channel_id=1, source_target_pairs={{0,192},{8,200},{16,208},{24,216},{32,224},{40,232},{48,240},{56,2... | collective-permute-start | bytes 1032200 | tf_op jit(solution)/shard_map/ppermute | solution.py:32
  163.4 21.3 %collective-permute-start.28 = (bf16[1344,128]{1,0:T(8,128)(2,1)S(1)}, bf16[1344,128]{1,0:T(8,128)(2,1)}, u32[]{:S(2)}, u32[]{:S(2)}) collective-permute-start(bf16[1344,128]{1,0:T(8,128)(2,1)S(1)} %get-tuple-element.80), channel_id=1, source_target_pairs={{0,128},{8,136},{16,144},{24,152},{32,160},{40,168},{48,176},{56,1... | collective-permute-start | bytes 1032200 | tf_op jit(solution)/shard_map/ppermute | solution.py:32
  166.6 18.2 %collective-permute-start.30 = (bf16[1344,128]{1,0:T(8,128)(2,1)}, bf16[1344,128]{1,0:T(8,128)(2,1)}, u32[]{:S(2)}, u32[]{:S(2)}) collective-permute-start(bf16[1344,128]{1,0:T(8,128)(2,1)} %get-tuple-element.78), channel_id=1, source_target_pairs={{0,64},{8,72},{16,80},{24,88},{32,96},{40,104},{48,112},{56,120},{... | collective-permute-start | bytes 1032200 | tf_op jit(solution)/shard_map/ppermute | solution.py:32
  169.1 2.9 %copy-start.11 = (bf16[1344,128]{1,0:T(8,128)(2,1)}, bf16[1344,128]{1,0:T(8,128)(2,1)S(1)}, u32[]{:S(2)}) copy-start(bf16[1344,128]{1,0:T(8,128)(2,1)S(1)} %collective-permute-done.26) | copy-start | bytes 1032196
  169.1 15.8 %collective-permute-start.31 = (bf16[1344,128]{1,0:T(8,128)(2,1)}, bf16[1344,128]{1,0:T(8,128)(2,1)}, u32[]{:S(2)}, u32[]{:S(2)}) collective-permute-start(bf16[1344,128]{1,0:T(8,128)(2,1)} %get-tuple-element.77), channel_id=1, source_target_pairs={{0,192},{8,200},{16,208},{24,216},{32,224},{40,232},{48,240},{56,2... | collective-permute-start | bytes 1032200 | tf_op jit(solution)/shard_map/ppermute | solution.py:32
  170.4 1.6 copy-start.6
  172.0 20.3 %collective-permute-start.32 = (bf16[1344,128]{1,0:T(8,128)(2,1)}, bf16[1344,128]{1,0:T(8,128)(2,1)}, u32[]{:S(2)}, u32[]{:S(2)}) collective-permute-start(bf16[1344,128]{1,0:T(8,128)(2,1)} %get-tuple-element.76), channel_id=1, source_target_pairs={{0,128},{8,136},{16,144},{24,152},{32,160},{40,168},{48,176},{56,1... | collective-permute-start | bytes 1032200 | tf_op jit(solution)/shard_map/ppermute | solution.py:32
  180.0 12.3 %copy-start.12 = (bf16[1344,128]{1,0:T(8,128)(2,1)S(1)}, bf16[1344,128]{1,0:T(8,128)(2,1)}, u32[]{:S(2)}) copy-start(bf16[1344,128]{1,0:T(8,128)(2,1)} %copy-done.11) | copy-start | bytes 1032196
  180.0 37.0 %all-to-all-start = ((bf16[4,64,5376]{2,1,0:T(8,128)(2,1)}), bf16[4,64,5376]{2,1,0:T(8,128)(2,1)}, u32[]{:S(2)}, u32[]{:S(2)}) async-start(bf16[4,64,5376]{2,1,0:T(8,128)(2,1)} %bitcast.91), calls=%async_computation | async-start | bytes 5505024 | tf_op jit(solution)/shard_map/all_to_all | solution.py:409
  195.0 18.8 %copy-start.13 = (s32[8]{0:T(128)S(1)}, s32[8]{0:T(128)}, u32[]{:S(2)}) copy-start(s32[8]{0:T(128)} %param.12) | copy-start | bytes 100
  195.0 20.1 %copy-start = (f32[168,1,512]{2,1,0:T(1,128)S(1)}, f32[168,1,512]{2,1,0:T(1,128)}, u32[]{:S(2)}) copy-start(f32[168,1,512]{2,1,0:T(1,128)} %param.9) | copy-start | bytes 1032196
  195.0 20.1 %copy-start.1 = (f32[168,1,512]{2,1,0:T(1,128)S(1)}, f32[168,1,512]{2,1,0:T(1,128)}, u32[]{:S(2)}) copy-start(f32[168,1,512]{2,1,0:T(1,128)} %param.10) | copy-start | bytes 1032196
  195.0 20.1 %copy-start.2 = (f32[168,1,512]{2,1,0:T(1,128)S(1)}, f32[168,1,512]{2,1,0:T(1,128)}, u32[]{:S(2)}) copy-start(f32[168,1,512]{2,1,0:T(1,128)} %param.11) | copy-start | bytes 1032196
  195.1 6.0 %collective-permute-start.35 = (bf16[336,256]{1,0:T(8,128)(2,1)S(1)}, bf16[336,256]{1,0:T(8,128)(2,1)S(1)}, u32[]{:S(2)}, u32[]{:S(2)}) collective-permute-start(bf16[336,256]{1,0:T(8,128)(2,1)S(1)} %get-tuple-element.85), channel_id=1, source_target_pairs={{0,32},{8,40},{16,48},{24,56},{32,0},{40,8},{48,16},{56,24},{64,96... | collective-permute-start | bytes 516104 | tf_op jit(solution)/shard_map/ppermute | solution.py:32
  195.2 9.1 %collective-permute-start.34 = (bf16[336,256]{1,0:T(8,128)(2,1)S(1)}, bf16[336,256]{1,0:T(8,128)(2,1)S(1)}, u32[]{:S(2)}, u32[]{:S(2)}) collective-permute-start(bf16[336,256]{1,0:T(8,128)(2,1)S(1)} %get-tuple-element.86), channel_id=1, source_target_pairs={{0,48},{8,56},{16,0},{24,8},{32,16},{40,24},{48,32},{56,40},{64,11... | collective-permute-start | bytes 516104 | tf_op jit(solution)/shard_map/ppermute | solution.py:32
  200.9 10.9 %collective-permute-start.33 = (bf16[336,256]{1,0:T(8,128)(2,1)S(1)}, bf16[336,256]{1,0:T(8,128)(2,1)S(1)}, u32[]{:S(2)}, u32[]{:S(2)}) collective-permute-start(bf16[336,256]{1,0:T(8,128)(2,1)S(1)} %get-tuple-element.84), channel_id=1, source_target_pairs={{0,16},{8,24},{16,32},{24,40},{32,48},{40,56},{48,0},{56,8},{64,80... | collective-permute-start | bytes 516104 | tf_op jit(solution)/shard_map/ppermute | solution.py:32
  211.9 3.2 %collective-permute-start.36 = (f32[168,256]{1,0:T(8,128)S(1)}, f32[168,256]{1,0:T(8,128)S(1)}, u32[]{:S(2)}, u32[]{:S(2)}) collective-permute-start(f32[168,256]{1,0:T(8,128)S(1)} %get-tuple-element.91), channel_id=1, source_target_pairs={{0,8},{8,0},{16,24},{24,16},{32,40},{40,32},{48,56},{56,48},{64,72... | collective-permute-start | bytes 516104 | tf_op jit(solution)/shard_map/ppermute | solution.py:32
